TPU v7x, 128 devices: a whole 4x4x4 slice. The times are simulated.
128 devices in a mesh: ty: 8 (over x, core), tx: 16 (over y, z).
Axes of the slice: x: 4, y: 4, z: 4, core: 2. Of those that a mesh axis runs over, the one named last changes fastest.
Arguments:
- gaussians: float32 [12288, 59, 128], P(('ty', 'tx')), may hold values from -18 to 22, as said below
- tile_lists: int32 [8, 16, 24], P('ty', 'tx'), may hold values from 0 to 12287, as said below
- tile_counts: int32 [8, 16], P('ty', 'tx'), may hold values from 3 to 24, as said below
- depth_order: int32 [12288], replicated, may hold values from 0 to 12287, as said below
- target: float32 [3, 256, 512], P(None, 'ty', 'tx'), may hold values from 0 to 1
Outputs:
- gaussian_grads: float32 [12288, 59, 128], P(('ty', 'tx'))
- loss: float32 [], replicated
Inputs may be any that keep to these rules, and one draw needn't show every extreme that they name: `tile_lists`: entries beyond a tile's count are arbitrary ranks. The live entries of a tile are rising depth ranks of blocks owned by devices in the tile's own row of ty (block b belongs to device b // 96 of ty+tx, ty slowest). At most 3 live entries of one tile name blocks of one owner; in every row some owner is named 3 times by every tile of the row. No block is live in two entries. `tile_counts`: some tile has 24 in every draw. A permutation: depth_order[r] is the block at depth rank r. `gaussians`: row 2 (Z) lies between 1.5 and 12, row 6 (the quaternion's w) between 0.5 and 1.5.
All inputs are finite; a program needn't handle non-finite values.
Results may differ from a plain program's by a relative error of at most 0.0003.
Values sent between devices are 32-bit elements; how exact they have to be, the bound alone decides.
A program may use at most 64 MiB of HBM per device.

v0:
```python
import jax
import jax.numpy as jnp
from jax import lax
from jax.sharding import PartitionSpec as P

GROUP = 4
CAP = 3


FOCAL = 1000.0
LOW_PASS = 0.3
STRUCT_WEIGHT = 0.2
LUMA_TERM = 0.0001
CONTRAST_TERM = 0.0009
ROBUST_TERM = 1e-06
HARMONIC_ZERO = 0.28209479177387814
HARMONIC_ONE = 0.4886025119029199
HARMONIC_TWO = (
    1.0925484305920792,
    -1.0925484305920792,
    0.31539156525252005,
    -1.0925484305920792,
    0.5462742152960396,
)
HARMONIC_THREE = (
    -0.5900435899266435,
    2.890611442640554,
    -0.4570457994644658,
    0.3731763325901154,
    -0.4570457994644658,
    1.445305721320277,
    -0.5900435899266435,
)


def extended(x, sides, width):
    for axis, dim in sides:
        size, length = (lax.axis_size(axis), x.shape[dim])
        up = [(i, (i + 1) % size) for i in range(size - 1)]
        down = [(j, i) for i, j in up]
        last = lax.slice_in_dim(x, length - width, length, axis=dim)
        first = lax.slice_in_dim(x, 0, width, axis=dim)
        before = lax.ppermute(last, axis, up)
        after = lax.ppermute(first, axis, down)
        x = jnp.concatenate([before, x, after], axis=dim)
    return x


def harmonics(dir_x, dir_y, dir_z):
    square_x = dir_x * dir_x
    square_y = dir_y * dir_y
    square_z = dir_z * dir_z
    pair_xy = dir_x * dir_y
    pair_yz = dir_y * dir_z
    pair_xz = dir_x * dir_z
    return jnp.stack(
        [
            HARMONIC_ZERO * jnp.ones_like(dir_x),
            -HARMONIC_ONE * dir_y,
            HARMONIC_ONE * dir_z,
            -HARMONIC_ONE * dir_x,
            HARMONIC_TWO[0] * pair_xy,
            HARMONIC_TWO[1] * pair_yz,
            HARMONIC_TWO[2] * (2.0 * square_z - square_x - square_y),
            HARMONIC_TWO[3] * pair_xz,
            HARMONIC_TWO[4] * (square_x - square_y),
            HARMONIC_THREE[0] * dir_y * (3.0 * square_x - square_y),
            HARMONIC_THREE[1] * pair_xy * dir_z,
            HARMONIC_THREE[2] * dir_y * (4.0 * square_z - square_x - square_y),
            HARMONIC_THREE[3] * dir_z * (2.0 * square_z - 3.0 * square_x - 3.0 * square_y),
            HARMONIC_THREE[4] * dir_x * (4.0 * square_z - square_x - square_y),
            HARMONIC_THREE[5] * dir_z * (square_x - square_y),
            HARMONIC_THREE[6] * dir_x * (square_x - 3.0 * square_y),
        ],
        axis=1,
    )


def project(raw, center_x, center_y):
    count_rows = raw.shape[0]
    block = raw.shape[2]
    mean_x, mean_y, mean_z = (raw[:, 0], raw[:, 1], raw[:, 2])
    scale = jnp.exp(raw[:, 3:6])
    quat = raw[:, 6:10] / jnp.sqrt(jnp.sum(raw[:, 6:10] * raw[:, 6:10], axis=1, keepdims=True))
    real, imag_i, imag_j, imag_k = (quat[:, 0], quat[:, 1], quat[:, 2], quat[:, 3])
    rotation = [
        [
            1.0 - 2.0 * (imag_j * imag_j + imag_k * imag_k),
            2.0 * (imag_i * imag_j - real * imag_k),
            2.0 * (imag_i * imag_k + real * imag_j),
        ],
        [
            2.0 * (imag_i * imag_j + real * imag_k),
            1.0 - 2.0 * (imag_i * imag_i + imag_k * imag_k),
            2.0 * (imag_j * imag_k - real * imag_i),
        ],
        [
            2.0 * (imag_i * imag_k - real * imag_j),
            2.0 * (imag_j * imag_k + real * imag_i),
            1.0 - 2.0 * (imag_i * imag_i + imag_j * imag_j),
        ],
    ]
    scaled = [[rotation[row][col] * scale[:, col] for col in range(3)] for row in range(3)]
    sigma = [
        [sum((scaled[row][col] * scaled[other][col] for col in range(3))) for other in range(3)]
        for row in range(3)
    ]
    inverse_z = 1.0 / mean_z
    jac_diag = FOCAL * inverse_z
    jac_xz = -FOCAL * mean_x * inverse_z * inverse_z
    jac_yz = -FOCAL * mean_y * inverse_z * inverse_z
    row_u = [jac_diag * sigma[0][col] + jac_xz * sigma[2][col] for col in range(3)]
    row_v = [jac_diag * sigma[1][col] + jac_yz * sigma[2][col] for col in range(3)]
    cov_uu = row_u[0] * jac_diag + row_u[2] * jac_xz + LOW_PASS
    cov_uv = row_u[1] * jac_diag + row_u[2] * jac_yz
    cov_vv = row_v[1] * jac_diag + row_v[2] * jac_yz + LOW_PASS
    determinant = cov_uu * cov_vv - cov_uv * cov_uv
    pos_u = FOCAL * mean_x * inverse_z + center_x
    pos_v = FOCAL * mean_y * inverse_z + center_y
    opacity = 0.99 * jax.nn.sigmoid(raw[:, 10])
    length = jnp.sqrt(mean_x * mean_x + mean_y * mean_y + mean_z * mean_z)
    basis = harmonics(mean_x / length, mean_y / length, mean_z / length)
    coeffs = raw[:, 11:59].reshape(count_rows, 16, 3, block)
    color = 0.5 + jnp.sum(coeffs * basis[:, :, None, :], axis=1)
    shape_rows = jnp.stack(
        [pos_u, pos_v, cov_vv / determinant, -cov_uv / determinant, cov_uu / determinant, opacity],
        axis=1,
    )
    return jnp.concatenate([shape_rows, color], axis=1)


def composite(flat, live, pixel_x, pixel_y):
    delta_x = pixel_x[None, :] - flat[0][:, None]
    delta_y = pixel_y[None, :] - flat[1][:, None]
    power = (
        flat[2][:, None] * delta_x * delta_x
        + 2.0 * flat[3][:, None] * delta_x * delta_y
        + flat[4][:, None] * delta_y * delta_y
    )
    alpha = (live * flat[5])[:, None] * jnp.exp(-0.5 * power)
    keep = jnp.log1p(-alpha)
    before = jnp.cumsum(keep, axis=0) - keep
    weight = alpha * jnp.exp(before)
    color = jnp.dot(
        flat[6:9], weight, precision=lax.Precision.HIGHEST, preferred_element_type=jnp.float32
    )
    return (color, jnp.sum(keep, axis=0))


def to_groups(slot_flat, live):
    lmax, fields, block = slot_flat.shape
    steps_total = lmax // GROUP
    groups = (
        slot_flat.reshape(steps_total, GROUP, fields, block)
        .transpose(0, 2, 1, 3)
        .reshape(steps_total, fields, GROUP * block)
    )
    live_groups = jnp.repeat(live.astype(jnp.float32), block).reshape(steps_total, GROUP * block)
    return (groups, live_groups)


def from_groups(grads, block):
    steps_total, fields, spread = grads.shape
    return (
        grads.reshape(steps_total, fields, GROUP, block)
        .transpose(0, 2, 1, 3)
        .reshape(steps_total * GROUP, fields, block)
    )


def render_forward(groups, live_groups, used, pixel_x, pixel_y):
    pixels = pixel_x.shape[0]

    def advance(index, carry):
        color, log_light, store = carry
        group_color, log_keep = composite(groups[index], live_groups[index], pixel_x, pixel_y)
        store = store.at[index].set(log_light)
        return (color + jnp.exp(log_light)[None, :] * group_color, log_light + log_keep, store)

    start = (
        jnp.zeros((3, pixels), jnp.float32),
        jnp.zeros((pixels,), jnp.float32),
        jnp.zeros((groups.shape[0], pixels), jnp.float32),
    )
    color, final_light, store = lax.fori_loop(0, used, advance, start)
    return (color, store)


def render_backward(groups, live_groups, used, store, pixel_x, pixel_y, color_grad):

    def retreat(step, carry):
        behind, grads = carry
        index = used - 1 - step
        live_now = live_groups[index]

        def shade(flat):
            return composite(flat, live_now, pixel_x, pixel_y)

        (group_color, log_keep), pull = jax.vjp(shade, groups[index])
        light = jnp.exp(store[index])
        passed = light * jnp.exp(log_keep)
        flat_grad = pull(
            (light[None, :] * color_grad, passed * jnp.sum(color_grad * behind, axis=0))
        )[0]
        behind = group_color + jnp.exp(log_keep)[None, :] * behind
        return (behind, grads.at[index].set(flat_grad))

    start = (jnp.zeros_like(color_grad), jnp.zeros_like(groups))
    return lax.fori_loop(0, used, retreat, start)[1]


def window_taps():
    offsets = jnp.arange(11, dtype=jnp.float32) - 5.0
    taps = jnp.exp(-offsets * offsets / 4.5)
    return taps / jnp.sum(taps)


def filtered(field, taps):
    rows = field.shape[-2] - 10
    cols = field.shape[-1] - 10
    sideways = sum((taps[shift] * field[..., :, shift : shift + cols] for shift in range(11)))
    return sum((taps[shift] * sideways[..., shift : shift + rows, :] for shift in range(11)))


def similarity(mean_a, mean_b, square_a, square_b, cross):
    var_a = square_a - mean_a * mean_a
    var_b = square_b - mean_b * mean_b
    covar = cross - mean_a * mean_b
    top = (2.0 * mean_a * mean_b + LUMA_TERM) * (2.0 * covar + CONTRAST_TERM)
    bottom = (mean_a * mean_a + mean_b * mean_b + LUMA_TERM) * (var_a + var_b + CONTRAST_TERM)
    return top / bottom


def moments(picture, goal, taps):
    return (
        filtered(picture, taps),
        filtered(goal, taps),
        filtered(picture * picture, taps),
        filtered(goal * goal, taps),
        filtered(picture * goal, taps),
    )


def per_device(gaussians, tile_lists, tile_counts, depth_order, target):
    owned = gaussians.shape[0]
    fields = gaussians.shape[1]
    block = gaussians.shape[2]
    lmax = tile_lists.shape[2]
    side = target.shape[1]
    across = lax.axis_size("tx")
    row_index = lax.axis_index("ty")
    col_index = lax.axis_index("tx")
    height = side * lax.axis_size("ty")
    width = side * across
    center_x = 0.5 * width
    center_y = 0.5 * height
    capacity = CAP

    def projector(raw):
        return project(raw, center_x, center_y)

    ranks = tile_lists.reshape(lmax)
    count = tile_counts.reshape(())
    live = jnp.arange(lmax, dtype=jnp.int32) < count
    blocks = depth_order[ranks]
    owner = blocks // owned - row_index * across
    local = blocks % owned
    hits = (
        (owner[:, None] == jnp.arange(across, dtype=jnp.int32)[None, :]) & live[:, None]
    ).astype(jnp.int32)
    position = jnp.sum((jnp.cumsum(hits, axis=0) - hits) * hits, axis=1)
    slot_index = jnp.where(live, owner * capacity + position, across * capacity)
    request = jnp.full((across * capacity,), -1, jnp.int32).at[slot_index].set(local, mode="drop")
    asked = lax.all_to_all(
        request.reshape(across, capacity), "tx", split_axis=0, concat_axis=0, tiled=True
    ).reshape(across * capacity)
    valid = asked >= 0
    served = gaussians[jnp.maximum(asked, 0)]
    pick = jnp.where(live, slot_index, 0)
    fetched = lax.all_to_all(
        served.reshape(across, capacity, fields, block),
        "tx",
        split_axis=0,
        concat_axis=0,
        tiled=True,
    ).reshape(across * capacity, fields, block)
    slot_flat, pull_raw = jax.vjp(projector, fetched[pick])
    offsets = jnp.arange(side * side, dtype=jnp.int32)
    pixel_x = (col_index * side + offsets % side).astype(jnp.float32) + 0.5
    pixel_y = (row_index * side + offsets // side).astype(jnp.float32) + 0.5
    groups, live_groups = to_groups(slot_flat, live)
    used = (count + GROUP - 1) // GROUP
    color, store = render_forward(groups, live_groups, used, pixel_x, pixel_y)
    image = color.reshape(3, side, side)
    taps = window_taps()
    stacked = jnp.stack([image, target])
    framed = extended(stacked, (("ty", 2), ("tx", 3)), 5)
    maps = moments(framed[0], framed[1], taps)
    score, pull_score = jax.vjp(similarity, *maps)
    parts = pull_score(jnp.full_like(score, -STRUCT_WEIGHT))
    coeffs = jnp.stack([parts[0], parts[2], parts[4]])
    spread = extended(coeffs, (("ty", 2), ("tx", 3)), 5)
    smoothed = filtered(spread, taps)
    gap = image - target
    robust = jnp.sqrt(gap * gap + ROBUST_TERM)
    local_total = jnp.sum((1.0 - STRUCT_WEIGHT) * robust + STRUCT_WEIGHT * (1.0 - score))
    image_grad = (
        smoothed[0]
        + 2.0 * image * smoothed[1]
        + target * smoothed[2]
        + (1.0 - STRUCT_WEIGHT) * gap / robust
    )
    total = lax.psum(local_total, ("ty", "tx"))
    flat_grads = render_backward(
        groups, live_groups, used, store, pixel_x, pixel_y, image_grad.reshape(3, side * side)
    )
    slot_grads = from_groups(flat_grads, block)
    raw_slot = pull_raw(slot_grads)[0]
    reply = (
        jnp.zeros((across * capacity, fields, block), jnp.float32)
        .at[slot_index]
        .set(raw_slot, mode="drop")
    )
    raw_grads = lax.all_to_all(
        reply.reshape(across, capacity, fields, block),
        "tx",
        split_axis=0,
        concat_axis=0,
        tiled=True,
    ).reshape(across * capacity, fields, block)
    destination = jnp.where(valid, asked, owned)
    gaussian_grads = jnp.zeros_like(gaussians).at[destination].add(raw_grads, mode="drop")
    return (gaussian_grads, total / (3.0 * height * width))


def solution(mesh):
    return jax.shard_map(
        per_device,
        mesh=mesh,
        in_specs=(
            P(("ty", "tx"), None, None),
            P("ty", "tx", None),
            P("ty", "tx"),
            P(),
            P(None, "ty", "tx"),
        ),
        out_specs=(P(("ty", "tx"), None, None), P()),
        check_vma=False,
    )
```

profile of v0, /device:TPU:1, one launch (start us, length us, event | category | flops | bytes accessed | tf_op | source)
XLA Modules:
  0.0 716.3 jit_solution(2859925716218883917)
XLA Ops:
  4.8 14.8 %all_to_all.19 = s32[16,1,3]{2,1,0:T(1,128)S(1)} all-to-all(s32[16,1,3]{2,1,0:T(1,128)S(1)} %bitcast.468), channel_id=1, replica_groups=mesh['ty'=8,'tx'=16] {'tx'}, dimensions={0} | all-to-all | bytes 384 | tf_op jit(solution)/shard_map/all_to_all | solution.py:274
  35.4 19.9 %all-to-all-done.1 = f32[16,3,59,128]{3,2,1,0:T(8,128)} async-done(((f32[16,3,59,128]{3,2,1,0:T(8,128)}), f32[16,3,59,128]{3,2,1,0:T(8,128)}, u32[]{:S(2)}, u32[]{:S(2)}) %all-to-all-start.1) | async-done | bytes 1450016 | tf_op jit(solution)/shard_map/all_to_all | solution.py:280
  66.7 88.2 %while.32 = (s32[]{:T(128)}, f32[3,1024]{1,0:T(4,128)S(1)}, f32[1024]{0:T(1024)S(1)}, f32[6,1024]{1,0:T(8,128)S(1)}, s32[]{:T(128)}, /*index=5*/f32[6,9,512]{2,1...) while((s32[]{:T(128)}, f32[3,1024]{1,0:T(4,128)S(1)}, ...), condition=%wide.region_10.11_spmd.clone, body=%wide.region_5.10_spmd.clone.sunk | while | flops 101230096 | bytes 25543560 | solution.py:185
  155.7 7.0 collective-permute-start
  168.7 15.7 %collective-permute-start.2 = (f32[2,3,42,5]{3,2,1,0:T(8,128)}, f32[2,3,42,5]{3,2,1,0:T(8,128)S(1)}, u32[]{:S(2)}, u32[]{:S(2)}) collective-permute-start(f32[2,3,42,5]{3,2,1,0:T(8,128)} %get-tuple-element.484), channel_id=1, source_target_pairs={{0,1},{1,2},{2,3},{3,4},{4,5},{5,6},{6,7},{7,8},{8,9},{9,10},{10,1... | collective-permute-start | bytes 15128 | tf_op jit(solution)/shard_map/ppermute | solution.py:43
  194.1 7.2 %fusion.154 = f32[3,42,32]{2,1,0:T(8,128)S(1)} fusion(f32[3,42,42]{2,1,0:T(8,128)S(1)} %get-tuple-element.482, f32[]{:T(128)} %bitcast.34, f32[]{:T(128)} %bitcast.33, f32[]{:T(128)} %bitcast.32, f32[]{:T(128)} %bitcast.31, f32[]{:T(128)} %bitcast.30, f32[]{:T(128)} %bitcast.29, f32[]{:T(128)} %bitcast.28, f32[]{:T(128)} %bitcast.27, f32[]{:T(128)} %bitcast.26, ...), kind=kLoop, calls=%fused_computation.284 | loop fusion | flops 84672 | bytes 193580 | tf_op jit(solution)/shard_map/add | solution.py:221
  201.3 7.2 %fusion.164 = f32[3,42,32]{2,1,0:T(8,128)S(1)} fusion(f32[3,42,42]{2,1,0:T(8,128)S(1)} %get-tuple-element.481, f32[]{:T(128)} %bitcast.34, f32[]{:T(128)} %bitcast.33, f32[]{:T(128)} %bitcast.32, f32[]{:T(128)} %bitcast.31, f32[]{:T(128)} %bitcast.30, f32[]{:T(128)} %bitcast.29, f32[]{:T(128)} %bitcast.28, f32[]{:T(128)} %bitcast.27, f32[]{:T(128)} %bitcast.26, ...), kind=kLoop, calls=%fused_computation.305 | loop fusion | flops 84672 | bytes 193580 | tf_op jit(solution)/shard_map/add | solution.py:221
  208.5 7.2 %fusion.144 = f32[3,42,32]{2,1,0:T(8,128)S(1)} fusion(f32[3,42,42]{2,1,0:T(8,128)S(1)} %get-tuple-element.483, f32[]{:T(128)} %bitcast.34, f32[]{:T(128)} %bitcast.33, f32[]{:T(128)} %bitcast.32, f32[]{:T(128)} %bitcast.31, f32[]{:T(128)} %bitcast.30, f32[]{:T(128)} %bitcast.29, f32[]{:T(128)} %bitcast.28, f32[]{:T(128)} %bitcast.27, f32[]{:T(128)} %bitcast.26, ...), kind=kLoop, calls=%fused_computation.263 | loop fusion | flops 84672 | bytes 193580 | tf_op jit(solution)/shard_map/add | solution.py:221
  215.7 7.2 %fusion.174 = f32[3,42,32]{2,1,0:T(8,128)S(1)} fusion(f32[3,42,42]{2,1,0:T(8,128)S(1)} %get-tuple-element.479, f32[]{:T(128)} %bitcast.34, f32[]{:T(128)} %bitcast.33, f32[]{:T(128)} %bitcast.32, f32[]{:T(128)} %bitcast.31, f32[]{:T(128)} %bitcast.30, f32[]{:T(128)} %bitcast.29, f32[]{:T(128)} %bitcast.28, f32[]{:T(128)} %bitcast.27, f32[]{:T(128)} %bitcast.26, ...), kind=kLoop, calls=%fused_computation.326 | loop fusion | flops 84672 | bytes 193580 | tf_op jit(solution)/shard_map/add | solution.py:221
  222.8 7.2 %fusion.184 = f32[3,42,32]{2,1,0:T(8,128)S(1)} fusion(f32[3,42,42]{2,1,0:T(8,128)S(1)} %get-tuple-element.480, f32[]{:T(128)} %bitcast.34, f32[]{:T(128)} %bitcast.33, f32[]{:T(128)} %bitcast.32, f32[]{:T(128)} %bitcast.31, f32[]{:T(128)} %bitcast.30, f32[]{:T(128)} %bitcast.29, f32[]{:T(128)} %bitcast.28, f32[]{:T(128)} %bitcast.27, f32[]{:T(128)} %bitcast.26, ...), kind=kLoop, calls=%fused_computation.348 | loop fusion | flops 84672 | bytes 193580 | tf_op jit(solution)/shard_map/add | solution.py:221
  230.0 8.0 %add_reduce_fusion = (f32[]{:T(128)}, f32[3,32,32]{2,1,0:T(8,128)S(1)}, f32[3,32,32]{2,1,0:T(8,128)S(1)}, f32[3,32,32]{2,1,0:T(8,128)S(1)}, f32[3,32,32]{2,1,0:T(8,128)S(1)}) fusion(f32[3,32,32]{2,1,0:T(8,128)S(1)} %reshape.610, f32[3,32,32]{2,1,0:T(8,128)S(1)} %copy-done.10, f32[3,42,32]{2,1,0:T(8,128)S(1)} %fusion.144, f32[]{:T(128)} %bitcast.34, ...), kind=kLoop, calls=%fused_computation.492 | loop fusion | flops 402431 | bytes 749616 | tf_op jit(solution)/shard_map/reduce_sum | solution.py:306
  261.1 7.5 %fusion.124 = f32[3,3,42,32]{3,2,1,0:T(8,128)S(1)} fusion(f32[3,3,42,37]{3,2,1,0:T(8,128)S(1)} %get-tuple-element.461, f32[3,3,42,37]{3,2,1,0:T(8,128)S(1)} %get-tuple-element.460, f32[]{:T(128)} %bitcast.34, f32[]{:T(128)} %bitcast.33, f32[]{:T(128)} %bitcast.32, f32[]{:T(128)} %bitcast.31, f32[]{:T(128)} %bitcast.30, f32[]{:T(128)} %bitcast.29, ...), kind=kLoop, calls=%fused_computation.215 | loop fusion | flops 302400 | bytes 580652 | tf_op jit(solution)/shard_map/add | solution.py:221
  268.6 7.1 fusion.134
  276.6 267.7 %while.33 = (s32[]{:T(128)}, f32[3,1024]{1,0:T(4,128)S(1)}, f32[6,9,512]{2,1,0:T(8,128)}, s32[]{:T(128)}, s32[]{:T(128)}, /*index=5*/f32[6,9,512]{2,1,0:T(8,128)...) while((s32[]{:T(128)}, f32[3,1024]{1,0:T(4,128)S(1)}, ...), condition=%wide.region_26.27_spmd.clone, body=%wide.region_12.0_spmd.clone.sunk | while | flops 245467152 | bytes 84695544 | solution.py:209
  308.2 5.9 fusion.394
  314.1 9.6 %fusion.395 = f32[1024,4,128]{0,1,2:T(4,128)S(1)} fusion(f32[1024,4,128]{0,2,1:T(8,128)S(1)} %bitcast.360), kind=kOutput, calls=%fused_computation.144.clone.1 | output fusion | flops 66584576 | bytes 4194304 | tf_op jit(solution)/shard_map/reduce-window.12
  357.9 5.9 fusion.394
  363.8 9.6 %fusion.395 = f32[1024,4,128]{0,1,2:T(4,128)S(1)} fusion(f32[1024,4,128]{0,2,1:T(8,128)S(1)} %bitcast.360), kind=kOutput, calls=%fused_computation.144.clone.1 | output fusion | flops 66584576 | bytes 4194304 | tf_op jit(solution)/shard_map/reduce-window.12
  413.5 9.6 %fusion.395 = f32[1024,4,128]{0,1,2:T(4,128)S(1)} fusion(f32[1024,4,128]{0,2,1:T(8,128)S(1)} %bitcast.360), kind=kOutput, calls=%fused_computation.144.clone.1 | output fusion | flops 66584576 | bytes 4194304 | tf_op jit(solution)/shard_map/reduce-window.12
  463.2 9.6 %fusion.395 = f32[1024,4,128]{0,1,2:T(4,128)S(1)} fusion(f32[1024,4,128]{0,2,1:T(8,128)S(1)} %bitcast.360), kind=kOutput, calls=%fused_computation.144.clone.1 | output fusion | flops 66584576 | bytes 4194304 | tf_op jit(solution)/shard_map/reduce-window.12
  512.9 9.6 %fusion.395 = f32[1024,4,128]{0,1,2:T(4,128)S(1)} fusion(f32[1024,4,128]{0,2,1:T(8,128)S(1)} %bitcast.360), kind=kOutput, calls=%fused_computation.144.clone.1 | output fusion | flops 66584576 | bytes 4194304 | tf_op jit(solution)/shard_map/reduce-window.12
  565.6 55.5 %all-to-all-start.2 = ((f32[16,3,59,128]{3,2,1,0:T(8,128)}), f32[16,3,59,128]{3,2,1,0:T(8,128)}, u32[]{:S(2)}, u32[]{:S(2)}) async-start(f32[16,3,59,128]{3,2,1,0:T(8,128)} %bitcast.361), calls=%async_computation.2 | async-start | bytes 3145728 | tf_op jit(solution)/shard_map/all_to_all | solution.py:324
  621.1 78.0 %psum.7 = f32[]{:T(128)} all-reduce(f32[]{:T(128)} %get-tuple-element.368), channel_id=1, replica_groups=mesh['ty'=8,'tx'=16] {'ty','tx'}, use_global_device_ids=true, to_apply=%region_32.33 | all-reduce | flops 1 | bytes 8 | tf_op jit(solution)/shard_map/psum | solution.py:313
  701.8 7.8 %scatter_fusion.1 = f32[96,59,128]{2,1,0:T(8,128)} fusion(f32[96,59,128]{2,1,0:T(8,128)} %broadcast_in_dim.60, s32[48]{0:T(128)S(1)} %copy-done.45, f32[48,59,128]{2,1,0:T(8,128)} %bitcast.44), kind=kCustom, calls=%fused_computation.5 | custom fusion | flops 362496 | bytes 4350144 | tf_op jit(solution)/shard_map/scatter-add | solution.py:332
  (571 shorter events, 373.7 us)
Async XLA Ops:
  0.6 20.8 %copy-start = (f32[96,59,128]{2,0,1:T(8,128)S(1)}, f32[96,59,128]{2,0,1:T(8,128)}, u32[]{:S(2)}) copy-start(f32[96,59,128]{2,0,1:T(8,128)} %param.13) | copy-start | bytes 8699908
  30.2 25.0 %all-to-all-start.1 = ((f32[16,3,59,128]{3,2,1,0:T(8,128)}), f32[16,3,59,128]{3,2,1,0:T(8,128)}, u32[]{:S(2)}, u32[]{:S(2)}) async-start(f32[16,3,59,128]{3,2,1,0:T(8,128)} %bitcast.362), calls=%async_computation.1 | async-start | bytes 3145728 | tf_op jit(solution)/shard_map/all_to_all | solution.py:280
  66.6 89.0 %copy-start.10 = (f32[3,32,32]{2,1,0:T(8,128)S(1)}, f32[3,32,32]{2,1,0:T(8,128)}, u32[]{:S(2)}) copy-start(f32[3,32,32]{2,1,0:T(8,128)} %param.17) | copy-start | bytes 36868
  155.6 52.9 %copy-start.20 = (f32[6,512]{1,0:T(8,128)}, f32[6,512]{1,0:T(8,128)S(1)}, u32[]{:S(2)}) copy-start(f32[6,512]{1,0:T(8,128)S(1)} %get-tuple-element.884) | copy-start | bytes 36868
  155.7 9.6 %collective-permute-start = (f32[2,3,5,32]{3,2,1,0:T(8,128)S(1)}, f32[2,3,5,32]{3,2,1,0:T(8,128)S(1)}, u32[]{:S(2)}, u32[]{:S(2)}) collective-permute-start(f32[2,3,5,32]{3,2,1,0:T(8,128)S(1)} %get-tuple-element.490), channel_id=1, source_target_pairs={{0,16},{16,32},{32,48},{48,64},{64,80},{80,96},{96,112},{1,17},{17... | collective-permute-start | bytes 11528 | tf_op jit(solution)/shard_map/ppermute | solution.py:43
  162.7 5.1 collective-permute-start.1
  168.7 18.8 %collective-permute-start.2 = (f32[2,3,42,5]{3,2,1,0:T(8,128)}, f32[2,3,42,5]{3,2,1,0:T(8,128)S(1)}, u32[]{:S(2)}, u32[]{:S(2)}) collective-permute-start(f32[2,3,42,5]{3,2,1,0:T(8,128)} %get-tuple-element.484), channel_id=1, source_target_pairs={{0,1},{1,2},{2,3},{3,4},{4,5},{5,6},{6,7},{7,8},{8,9},{9,10},{10,1... | collective-permute-start | bytes 15128 | tf_op jit(solution)/shard_map/ppermute | solution.py:43
  184.3 8.7 %collective-permute-start.3 = (f32[2,3,42,5]{3,2,1,0:T(8,128)S(1)}, f32[2,3,42,5]{3,2,1,0:T(8,128)}, u32[]{:S(2)}, u32[]{:S(2)}) collective-permute-start(f32[2,3,42,5]{3,2,1,0:T(8,128)S(1)} %get-tuple-element.485), channel_id=1, source_target_pairs={{1,0},{2,1},{3,2},{4,3},{5,4},{6,5},{7,6},{8,7},{9,8},{10,9},{11,1... | collective-permute-start | bytes 15128 | tf_op jit(solution)/shard_map/ppermute | solution.py:44
  238.1 6.1 collective-permute-start.4
  242.2 5.3 collective-permute-start.5
  248.3 6.7 collective-permute-start.6
  251.9 7.9 %collective-permute-start.7 = (f32[3,3,42,5]{3,2,1,0:T(8,128)}, f32[3,3,42,5]{3,2,1,0:T(8,128)}, u32[]{:S(2)}, u32[]{:S(2)}) collective-permute-start(f32[3,3,42,5]{3,2,1,0:T(8,128)} %get-tuple-element.463), channel_id=1, source_target_pairs={{1,0},{2,1},{3,2},{4,3},{5,4},{6,5},{7,6},{8,7},{9,8},{10,9},{11,1... | collective-permute-start | bytes 22688 | tf_op jit(solution)/shard_map/ppermute | solution.py:44
  261.1 15.5 %copy-start.41 = (s32[3]{0:T(128)S(1)}, s32[3]{0:T(128)}, u32[]{:S(2)}) copy-start(s32[3]{0:T(128)} %constant.228.clone.2) | copy-start | bytes 40
  544.3 12.4 %copy-start.7 = (f32[24,48,128]{2,0,1:T(8,128)S(1)}, f32[24,48,128]{2,0,1:T(8,128)}, u32[]{:S(2)}) copy-start(f32[24,48,128]{2,0,1:T(8,128)} %copy-done.6) | copy-start | bytes 1769476
  547.5 10.2 %copy-start.24 = (f32[24,1,128]{2,0,1:T(8,128)S(1)}, f32[24,1,128]{2,0,1:T(8,128)}, u32[]{:S(2)}) copy-start(f32[24,1,128]{2,0,1:T(8,128)} %get-tuple-element.504) | copy-start | bytes 36868
  547.5 10.2 %copy-start.25 = (f32[24,1,128]{2,0,1:T(8,128)S(1)}, f32[24,1,128]{2,0,1:T(8,128)}, u32[]{:S(2)}) copy-start(f32[24,1,128]{2,0,1:T(8,128)} %get-tuple-element.509) | copy-start | bytes 36868
  547.5 10.2 %copy-start.26 = (f32[24,1,128]{2,0,1:T(8,128)S(1)}, f32[24,1,128]{2,0,1:T(8,128)}, u32[]{:S(2)}) copy-start(f32[24,1,128]{2,0,1:T(8,128)} %get-tuple-element.510) | copy-start | bytes 36868
  547.5 10.2 %copy-start.30 = (f32[24,1,128]{2,0,1:T(8,128)S(1)}, f32[24,1,128]{2,0,1:T(8,128)}, u32[]{:S(2)}) copy-start(f32[24,1,128]{2,0,1:T(8,128)} %get-tuple-element.506) | copy-start | bytes 36868
  547.6 10.2 %copy-start.31 = (f32[24,1,128]{2,0,1:T(8,128)S(1)}, f32[24,1,128]{2,0,1:T(8,128)}, u32[]{:S(2)}) copy-start(f32[24,1,128]{2,0,1:T(8,128)} %get-tuple-element.507) | copy-start | bytes 36868
  547.6 10.2 %copy-start.32 = (f32[24,1,128]{2,0,1:T(8,128)S(1)}, f32[24,1,128]{2,0,1:T(8,128)}, u32[]{:S(2)}) copy-start(f32[24,1,128]{2,0,1:T(8,128)} %get-tuple-element.519) | copy-start | bytes 36868
  547.6 10.2 %copy-start.33 = (f32[24,1,128]{2,0,1:T(8,128)S(1)}, f32[24,1,128]{2,0,1:T(8,128)}, u32[]{:S(2)}) copy-start(f32[24,1,128]{2,0,1:T(8,128)} %get-tuple-element.522) | copy-start | bytes 36868
  547.6 10.2 %copy-start.40 = (f32[24,1,128]{2,0,1:T(8,128)S(1)}, f32[24,1,128]{2,0,1:T(8,128)}, u32[]{:S(2)}) copy-start(f32[24,1,128]{2,0,1:T(8,128)} %get-tuple-element.502) | copy-start | bytes 36868
  565.6 134.2 %all-to-all-start.2 = ((f32[16,3,59,128]{3,2,1,0:T(8,128)}), f32[16,3,59,128]{3,2,1,0:T(8,128)}, u32[]{:S(2)}, u32[]{:S(2)}) async-start(f32[16,3,59,128]{3,2,1,0:T(8,128)} %bitcast.361), calls=%async_computation.2 | async-start | bytes 3145728 | tf_op jit(solution)/shard_map/all_to_all | solution.py:324
  621.1 80.7 %copy-start.45 = (s32[48]{0:T(128)S(1)}, s32[48]{0:T(128)}, u32[]{:S(2)}) copy-start(s32[48]{0:T(128)} %get-tuple-element.549) | copy-start | bytes 580
  (52 other events, 186.0 us)
where the time goes:
time: 727 us; the launch traced here: 716 us
  other arithmetic  297 us (41%)
  local copies, waits for them, and re-layouts  104 us (14%)
  starting transfers between devices  96.8 us (13%)
  blocking collectives  92.8 us (13%)
  matrix products  61.6 us (8%)
  waiting for transfers between devices  39 us (5%)
  loops' own time  20.8 us (3%)
    another operation x61, other arithmetic  125 us
    psum x1, blocking collectives, per_device(): total = lax.psum(local_total, ('ty', 'tx'))  78 us
    dot_general x20, matrix products, composite(): jnp.dot(flat[6:9], weight, precision=lax.Precision.HIGHEST, preferred_ele...  61.6 us
    all_to_all x1, starting transfers between devices, per_device(): lax.all_to_all(reply.reshape(across, capacity, fields, block), 'tx', spli...  55.5 us
    add x6, other arithmetic, filtered(): sum((taps[shift] * field[..., :, shift:shift + cols] for shift in range(1...  43.4 us
    ppermute x4, starting transfers between devices, extended(): before = lax.ppermute(last, axis, up)  30.4 us
    reduce_sum x10, other arithmetic, composite(): return (color, jnp.sum(keep, axis=0))  26.6 us
    another operation x48, local copies, waits for them, and re-layouts  25.9 us
  transfers between devices with their start and end apart: 10, of which 7 were waited for; matrix products, arithmetic and copies ran while one was open for 0% of the time, Pallas kernels for 0%

commit v1 on v0

v1 whole, which is shorter than its diff:
```python
import functools
import math

import jax
import jax.numpy as jnp
import numpy as np
from jax import lax
from jax.experimental import pallas as pl
from jax.experimental.pallas import tpu as pltpu
from jax.sharding import PartitionSpec as P

CAP = 3
SLOT = 8
LMAX = 24
BLOCK = 128
SIDE = 32
PIX = SIDE * SIDE
UNIT = 8
UNITS = LMAX // UNIT
ROWS = UNIT * BLOCK
CHUNK = 128
CHUNKS = ROWS // CHUNK
STEPS = CHUNK // UNIT
FIELDS = 59
WIDE = 9 * BLOCK

FOCAL = 1000.0
LOW_PASS = 0.3
STRUCT_WEIGHT = 0.2
LUMA_TERM = 0.0001
CONTRAST_TERM = 0.0009
ROBUST_TERM = 1e-06
LOG2E = math.log2(math.e)
HARMONIC_ZERO = 0.28209479177387814
HARMONIC_ONE = 0.4886025119029199
HARMONIC_TWO = (
    1.0925484305920792,
    -1.0925484305920792,
    0.31539156525252005,
    -1.0925484305920792,
    0.5462742152960396,
)
HARMONIC_THREE = (
    -0.5900435899266435,
    2.890611442640554,
    -0.4570457994644658,
    0.3731763325901154,
    -0.4570457994644658,
    1.445305721320277,
    -0.5900435899266435,
)
VMEM = pltpu.VMEM
F32 = jnp.float32
BF16 = jnp.bfloat16


def harmonics(dir_x, dir_y, dir_z):
    square_x = dir_x * dir_x
    square_y = dir_y * dir_y
    square_z = dir_z * dir_z
    pair_xy = dir_x * dir_y
    pair_yz = dir_y * dir_z
    pair_xz = dir_x * dir_z
    return [
        HARMONIC_ZERO * jnp.ones_like(dir_x),
        -HARMONIC_ONE * dir_y,
        HARMONIC_ONE * dir_z,
        -HARMONIC_ONE * dir_x,
        HARMONIC_TWO[0] * pair_xy,
        HARMONIC_TWO[1] * pair_yz,
        HARMONIC_TWO[2] * (2.0 * square_z - square_x - square_y),
        HARMONIC_TWO[3] * pair_xz,
        HARMONIC_TWO[4] * (square_x - square_y),
        HARMONIC_THREE[0] * dir_y * (3.0 * square_x - square_y),
        HARMONIC_THREE[1] * pair_xy * dir_z,
        HARMONIC_THREE[2] * dir_y * (4.0 * square_z - square_x - square_y),
        HARMONIC_THREE[3] * dir_z * (2.0 * square_z - 3.0 * square_x - 3.0 * square_y),
        HARMONIC_THREE[4] * dir_x * (4.0 * square_z - square_x - square_y),
        HARMONIC_THREE[5] * dir_z * (square_x - square_y),
        HARMONIC_THREE[6] * dir_x * (square_x - 3.0 * square_y),
    ]


def shape_of(center_x, center_y, mean_x, mean_y, mean_z, s0, s1, s2, q0, q1, q2, q3, logit):
    scale = [jnp.exp(s0), jnp.exp(s1), jnp.exp(s2)]
    norm = 1.0 / jnp.sqrt(q0 * q0 + q1 * q1 + q2 * q2 + q3 * q3)
    real, imag_i, imag_j, imag_k = q0 * norm, q1 * norm, q2 * norm, q3 * norm
    rotation = [
        [
            1.0 - 2.0 * (imag_j * imag_j + imag_k * imag_k),
            2.0 * (imag_i * imag_j - real * imag_k),
            2.0 * (imag_i * imag_k + real * imag_j),
        ],
        [
            2.0 * (imag_i * imag_j + real * imag_k),
            1.0 - 2.0 * (imag_i * imag_i + imag_k * imag_k),
            2.0 * (imag_j * imag_k - real * imag_i),
        ],
        [
            2.0 * (imag_i * imag_k - real * imag_j),
            2.0 * (imag_j * imag_k + real * imag_i),
            1.0 - 2.0 * (imag_i * imag_i + imag_j * imag_j),
        ],
    ]
    scaled = [[rotation[row][col] * scale[col] for col in range(3)] for row in range(3)]

    def sigma(row, other):
        a, b = scaled[row], scaled[other]
        return a[0] * b[0] + a[1] * b[1] + a[2] * b[2]

    xx, xy, xz = sigma(0, 0), sigma(0, 1), sigma(0, 2)
    yy, yz, zz = sigma(1, 1), sigma(1, 2), sigma(2, 2)
    inverse_z = 1.0 / mean_z
    diag = FOCAL * inverse_z
    jac_xz = -FOCAL * mean_x * inverse_z * inverse_z
    jac_yz = -FOCAL * mean_y * inverse_z * inverse_z
    u0, u1, u2 = diag * xx + jac_xz * xz, diag * xy + jac_xz * yz, diag * xz + jac_xz * zz
    v1, v2 = diag * yy + jac_yz * yz, diag * yz + jac_yz * zz
    cov_uu = u0 * diag + u2 * jac_xz + LOW_PASS
    cov_uv = u1 * diag + u2 * jac_yz
    cov_vv = v1 * diag + v2 * jac_yz + LOW_PASS
    inverse = 1.0 / (cov_uu * cov_vv - cov_uv * cov_uv)
    pos_u = FOCAL * mean_x * inverse_z + center_x
    pos_v = FOCAL * mean_y * inverse_z + center_y
    log_opacity = jnp.log(0.99 / (1.0 + jnp.exp(-logit)))
    return pos_u, pos_v, cov_vv * inverse, -cov_uv * inverse, cov_uu * inverse, log_opacity


def basis_of(mean_x, mean_y, mean_z):
    inverse = 1.0 / jnp.sqrt(mean_x * mean_x + mean_y * mean_y + mean_z * mean_z)
    return harmonics(mean_x * inverse, mean_y * inverse, mean_z * inverse)


def pieces(x, count):
    out = []
    for left in range(count):
        part = x.astype(BF16).astype(F32)
        out.append(part)
        if left < count - 1:
            x = x - part
    return out


def project_kernel(owned, center, ranks, count, order, place, g_ref, out_ref, req_ref, slot_ref, used):
    step = pl.program_id(0)

    @pl.when(step == 0)
    def _():
        req_ref[...] = jnp.full_like(req_ref, -1)
        first = place[0]
        for o in range(req_ref.shape[0] // SLOT):
            used[o] = 0

        def put(k, carry):
            block = order[ranks[k]]
            home = block // owned
            owner = home - first
            local = block - home * owned

            @pl.when(k < count[0])
            def _():
                row = owner * SLOT + used[owner]
                used[owner] = used[owner] + 1
                slot_ref[k] = row
                req_ref[pl.ds(row, 1), :] = jnp.full((1, BLOCK), local, jnp.int32)

            @pl.when(k >= count[0])
            def _():
                slot_ref[k] = SLOT - 1

            return carry

        lax.fori_loop(0, LMAX, put, 0)

    field = [g_ref[:, f, :] for f in range(11)]
    shape = shape_of(center[0], center[1], *field)
    basis = basis_of(*field[:3])
    for f in range(6):
        out_ref[:, f * BLOCK : (f + 1) * BLOCK] = shape[f]
    for ch in range(3):
        color = jnp.full((UNIT, BLOCK), 0.5, F32)
        for m in range(16):
            color = color + g_ref[:, 11 + 3 * m + ch, :] * basis[m]
        out_ref[:, (6 + ch) * BLOCK : (7 + ch) * BLOCK] = color


def project_blocks(gaussians, ranks, count, order, place, center, peers):
    owned = gaussians.shape[0]
    smem = pl.BlockSpec(memory_space=pltpu.SMEM)
    return pl.pallas_call(
        functools.partial(project_kernel, owned, center),
        grid=(owned // UNIT,),
        in_specs=[smem, smem, smem, smem, pl.BlockSpec((UNIT, FIELDS, BLOCK), lambda i: (i, 0, 0))],
        out_specs=[
            pl.BlockSpec((UNIT, WIDE), lambda i: (i, 0)),
            pl.BlockSpec((peers * SLOT, BLOCK), lambda i: (0, 0)),
            smem,
        ],
        out_shape=[
            jax.ShapeDtypeStruct((owned, WIDE), F32),
            jax.ShapeDtypeStruct((peers * SLOT, BLOCK), jnp.int32),
            jax.ShapeDtypeStruct((LMAX,), jnp.int32),
        ],
        scratch_shapes=[pltpu.SMEM((peers,), jnp.int32)],
        name="project",
    )(ranks, count, order, place, gaussians)


def features():
    offset = np.arange(PIX)
    x = (offset % SIDE - SIDE // 2).astype(np.float32)
    y = (offset // SIDE - SIDE // 2).astype(np.float32)
    six = np.stack([np.ones_like(x), x, y, x * x, x * y, y * y])
    ahead = np.zeros((32, PIX), np.float32)
    for piece in range(3):
        ahead[6 * piece : 6 * piece + 6] = six
    back = np.zeros((16, PIX), np.float32)
    back[:6] = six
    return jnp.asarray(ahead, BF16), jnp.asarray(back, BF16)


def load_entries(slot_ref, recv_ref, ent_ref):
    for k in range(LMAX):
        ent_ref[k : k + 1, :] = recv_ref[pl.ds(slot_ref[k], 1), :]


def build_rows(place, count, ent_ref, field_ref, row_ref):
    mid_x = place[2].astype(F32)
    mid_y = place[1].astype(F32)
    mid_x = mid_x * SIDE + (SIDE // 2 + 0.5)
    mid_y = mid_y * SIDE + (SIDE // 2 + 0.5)
    field_ref[...] = jnp.zeros_like(field_ref)
    for unit in range(UNITS):
        rows = slice(unit * UNIT, (unit + 1) * UNIT)
        u, v, a, b, c, log_o, r0, r1, r2 = [
            ent_ref[rows, f * BLOCK : (f + 1) * BLOCK] for f in range(9)
        ]
        entry = lax.broadcasted_iota(jnp.int32, (UNIT, BLOCK), 0) + unit * UNIT
        live = entry < count[0]
        du, dv = u - mid_x, v - mid_y
        k = -0.5 * LOG2E
        mix_u, mix_v = a * du + b * dv, b * du + c * dv
        coefs = [
            jnp.where(live, k * (mix_u * du + mix_v * dv) + LOG2E * log_o, -1e4),
            -2.0 * k * mix_u,
            -2.0 * k * mix_v,
            k * a,
            2.0 * k * b,
            k * c,
        ]
        coefs = coefs[:1] + [jnp.where(live, q, 0.0) for q in coefs[1:]]
        color = [jnp.where(live, r, 0.0) for r in (r0, r1, r2)]
        split = [pieces(q, 3) for q in coefs]
        shade = [pieces(r, 2) for r in color]
        columns = [split[f][piece] for piece in range(3) for f in range(6)]
        columns += [s[0] for s in shade] + [s[0] for s in shade] + [s[1] for s in shade]
        columns += color
        for f, column in enumerate(columns):
            field_ref[f * UNIT : (f + 1) * UNIT, :] = column
        for s in range(UNIT):
            table = field_ref[pl.ds(s, 32, stride=UNIT), :].T
            table = jnp.concatenate([table, jnp.zeros((BLOCK, BLOCK - 32), F32)], axis=1)
            row_ref[pl.ds(unit * ROWS + s, BLOCK, stride=UNIT), :] = table


def exponent_chunk(row_ref, ahead, chunk, alpha_ref):
    base = pl.multiple_of(chunk * CHUNK, CHUNK)
    rows = row_ref[pl.ds(base, CHUNK), :][:, :32].astype(BF16)
    alpha_ref[...] = jnp.exp2(jnp.dot(rows, ahead, preferred_element_type=F32))


def scan_chunk(row_ref, chunk, alpha_ref, carry):
    light, c0, c1, c2 = carry
    base = pl.multiple_of(chunk * CHUNK, CHUNK)
    for i in range(STEPS):
        alpha = alpha_ref[i * UNIT : (i + 1) * UNIT, :]
        shade = row_ref[pl.ds(base + i * UNIT, UNIT), :]
        weight = alpha * light
        light = light - weight
        c0 = c0 + shade[:, 27:28] * weight
        c1 = c1 + shade[:, 28:29] * weight
        c2 = c2 + shade[:, 29:30] * weight
    return light, c0, c1, c2


def forward_kernel(slot_ref, count, place, ahead_ref, recv_ref, image_ref, light_ref, color_ref,
                   row_ref, ent_ref, field_ref, even_ref, odd_ref):
    load_entries(slot_ref, recv_ref, ent_ref)
    build_rows(place, count, ent_ref, field_ref, row_ref)
    ahead = ahead_ref[...]
    last = UNITS * CHUNKS - 1
    exponent_chunk(row_ref, ahead, 0, even_ref)
    for unit in range(UNITS):
        zero = jnp.zeros((UNIT, PIX), F32)

        def advance(step, carry):
            chunk = unit * CHUNKS + 2 * step
            exponent_chunk(row_ref, ahead, chunk + 1, odd_ref)
            carry = scan_chunk(row_ref, chunk, even_ref, carry)
            exponent_chunk(row_ref, ahead, jnp.minimum(chunk + 2, last), even_ref)
            return scan_chunk(row_ref, chunk + 1, odd_ref, carry)

        light, c0, c1, c2 = lax.fori_loop(0, CHUNKS // 2, advance, (zero + 1.0, zero, zero, zero))
        rows = slice(unit * UNIT, (unit + 1) * UNIT)
        light_ref[rows, :] = light
        color_ref[0, rows, :] = c0
        color_ref[1, rows, :] = c1
        color_ref[2, rows, :] = c2
    light = jnp.ones((1, PIX), F32)
    image = [jnp.zeros((1, PIX), F32) for _ in range(3)]
    for k in range(LMAX):
        for ch in range(3):
            image[ch] = image[ch] + light * color_ref[ch, k : k + 1, :]
        light = light * light_ref[k : k + 1, :]
    for ch in range(3):
        for j in range(8):
            image_ref[ch, j : j + 1, :] = image[ch][:, j * BLOCK : (j + 1) * BLOCK]


def render(slots, count, place, ahead, recv):
    smem = pl.BlockSpec(memory_space=pltpu.SMEM)
    vmem = pl.BlockSpec(memory_space=pltpu.VMEM)
    return pl.pallas_call(
        forward_kernel,
        in_specs=[smem, smem, smem, vmem, vmem],
        out_specs=[vmem, vmem, vmem],
        out_shape=[
            jax.ShapeDtypeStruct((3, 8, BLOCK), F32),
            jax.ShapeDtypeStruct((LMAX, PIX), F32),
            jax.ShapeDtypeStruct((3, LMAX, PIX), F32),
        ],
        scratch_shapes=[
            VMEM((UNITS * ROWS, BLOCK), F32),
            VMEM((LMAX, WIDE), F32),
            VMEM((32 * UNIT, BLOCK), F32),
            VMEM((CHUNK, PIX), F32),
            VMEM((CHUNK, PIX), F32),
        ],
        name="render",
    )(slots, count, place, ahead, recv)


def long_row(ref, ch):
    return jnp.concatenate([ref[ch, j : j + 1, :] for j in range(8)], axis=1)


NT = (((1,), (1,)), ((), ()))


def backward_kernel(slot_ref, count, place, ahead_ref, back_ref, recv_ref, light_ref, color_ref, grad_ref,
                    out_ref, row_ref, ent_ref, field_ref, alpha_ref, weight_ref, shade_ref, start_ref,
                    behind_ref, moment_ref, result_ref):
    load_entries(slot_ref, recv_ref, ent_ref)
    build_rows(place, count, ent_ref, field_ref, row_ref)
    ahead = ahead_ref[...]
    grad = [long_row(grad_ref, ch) for ch in range(3)]
    high = [g.astype(BF16).astype(F32) for g in grad]
    low = [g - h for g, h in zip(grad, high)]
    zero = [jnp.zeros((1, PIX), F32)]
    mixed = jnp.concatenate(zero * 18 + high + low + high + zero * 5, axis=0).astype(BF16)
    tail = jnp.concatenate(zero * 8 + high + low + zero * 2, axis=0).astype(BF16)
    back = back_ref[...]

    light = jnp.ones((1, PIX), F32)
    for k in range(LMAX):
        start_ref[k : k + 1, :] = light
        light = light * light_ref[k : k + 1, :]
    behind = jnp.zeros((1, PIX), F32)
    for k in reversed(range(LMAX)):
        behind_ref[k : k + 1, :] = behind
        own = sum(grad[ch] * color_ref[ch, k : k + 1, :] for ch in range(3))
        behind = own + light_ref[k : k + 1, :] * behind

    def unit_pass(unit, carry):
        rows = pl.ds(pl.multiple_of(unit * UNIT, UNIT), UNIT)

        def recompute(chunk, light):
            base = pl.multiple_of(chunk * CHUNK, CHUNK)
            total = pl.multiple_of(unit * ROWS + base, CHUNK)
            packed = row_ref[pl.ds(total, CHUNK), :][:, :32].astype(BF16)
            alpha_ref[pl.ds(base, CHUNK), :] = jnp.exp2(jnp.dot(packed, ahead, preferred_element_type=F32))
            for i in range(STEPS):
                weight = alpha_ref[pl.ds(base + i * UNIT, UNIT), :] * light
                light = light - weight
                weight_ref[pl.ds(base + i * UNIT, UNIT), :] = weight
            return light

        lax.fori_loop(0, CHUNKS, recompute, start_ref[rows, :])

        def retreat(step, behind):
            base = pl.multiple_of((CHUNKS - 1 - step) * CHUNK, CHUNK)
            total = pl.multiple_of(unit * ROWS + base, CHUNK)
            packed = row_ref[pl.ds(total, CHUNK), :][:, :32].astype(BF16)
            shade_ref[...] = jnp.dot(packed, mixed, preferred_element_type=F32)
            for i in reversed(range(STEPS)):
                here = slice(i * UNIT, (i + 1) * UNIT)
                gap = shade_ref[here, :] - behind
                behind = behind + alpha_ref[pl.ds(base + i * UNIT, UNIT), :] * gap
                shade_ref[here, :] = weight_ref[pl.ds(base + i * UNIT, UNIT), :] * gap
            slope = shade_ref[...]
            weight = weight_ref[pl.ds(base, CHUNK), :]
            slope_high = slope.astype(BF16)
            slope_low = (slope - slope_high.astype(F32)).astype(BF16)
            weight_high = weight.astype(BF16)
            weight_low = (weight - weight_high.astype(F32)).astype(BF16)
            moment = lax.dot_general(slope_high, back, NT, preferred_element_type=F32)
            moment += lax.dot_general(slope_low, back, NT, preferred_element_type=F32)
            moment += lax.dot_general(weight_high, tail, NT, preferred_element_type=F32)
            moment += lax.dot_general(weight_low, tail, NT, preferred_element_type=F32)
            moment_ref[pl.ds(total, CHUNK), 0:16] = moment
            return behind

        lax.fori_loop(0, CHUNKS, retreat, behind_ref[rows, :])
        return carry

    moment_ref[...] = jnp.zeros_like(moment_ref)
    lax.fori_loop(0, UNITS, unit_pass, 0)

    mid_x = place[2].astype(F32) * SIDE + (SIDE // 2 + 0.5)
    mid_y = place[1].astype(F32) * SIDE + (SIDE // 2 + 0.5)
    for unit in range(UNITS):
        rows = slice(unit * UNIT, (unit + 1) * UNIT)
        for s in range(UNIT):
            table = moment_ref[pl.ds(unit * ROWS + s, BLOCK, stride=UNIT), :].T
            field_ref[pl.ds(s, 16, stride=UNIT), :] = table[:16]
        m = [field_ref[f * UNIT : (f + 1) * UNIT, :] for f in range(14)]
        u, v, a, b, c = [ent_ref[rows, f * BLOCK : (f + 1) * BLOCK] for f in range(5)]
        du, dv = u - mid_x, v - mid_y
        near_x, near_y = m[1] - du * m[0], m[2] - dv * m[0]
        values = [
            a * near_x + b * near_y,
            b * near_x + c * near_y,
            -0.5 * (m[3] - du * (m[1] + near_x)),
            -(m[4] - du * m[2] - dv * near_x),
            -0.5 * (m[5] - dv * (m[2] + near_y)),
            m[0],
            m[8] + m[11],
            m[9] + m[12],
            m[10] + m[13],
        ]
        for f, value in enumerate(values):
            result_ref[rows, f * BLOCK : (f + 1) * BLOCK] = value
    for k in range(LMAX):
        out_ref[pl.ds(slot_ref[k], 1), :] = result_ref[k : k + 1, :]


def render_gradient(slots, count, place, ahead, back, recv, light, color, grad):
    smem = pl.BlockSpec(memory_space=pltpu.SMEM)
    vmem = pl.BlockSpec(memory_space=pltpu.VMEM)
    return pl.pallas_call(
        backward_kernel,
        in_specs=[smem, smem, smem] + [vmem] * 6,
        out_specs=vmem,
        out_shape=jax.ShapeDtypeStruct(recv.shape, F32),
        scratch_shapes=[
            VMEM((UNITS * ROWS, BLOCK), F32),
            VMEM((LMAX, WIDE), F32),
            VMEM((32 * UNIT, BLOCK), F32),
            VMEM((ROWS, PIX), F32),
            VMEM((ROWS, PIX), F32),
            VMEM((CHUNK, PIX), F32),
            VMEM((LMAX, PIX), F32),
            VMEM((LMAX, PIX), F32),
            VMEM((UNITS * ROWS, BLOCK), F32),
            VMEM((LMAX, WIDE), F32),
        ],
        name="render_gradient",
    )(slots, count, place, ahead, back, recv, light, color, grad)


def pull_kernel(center, req_ref, back_ref, g_ref, out_ref, dense_ref):
    step = pl.program_id(0)

    @pl.when(step == 0)
    def _():
        owned = dense_ref.shape[0]
        req = req_ref[...]
        lane = lax.broadcasted_iota(jnp.int32, req.shape, 1)
        chosen = jnp.where(req == lane, 1.0, 0.0).T[:owned].astype(BF16)
        asked = req >= 0
        for f in range(9):
            cols = slice(f * BLOCK, (f + 1) * BLOCK)
            value = jnp.where(asked, back_ref[:, cols], 0.0)
            dense_ref[:, cols] = sum(
                jnp.dot(chosen, part.astype(BF16), preferred_element_type=F32) for part in pieces(value, 3)
            )

    rows = pl.ds(pl.multiple_of(step * UNIT, UNIT), UNIT)
    cot = [dense_ref[rows, f * BLOCK : (f + 1) * BLOCK] for f in range(9)]
    field = [g_ref[:, f, :] for f in range(11)]
    _, pull = jax.vjp(functools.partial(shape_of, center[0], center[1]), *field)
    grads = list(pull(tuple(cot[:6])))
    basis, pull_basis = jax.vjp(basis_of, *field[:3])
    basis_cot = []
    for m in range(16):
        total = jnp.zeros((UNIT, BLOCK), F32)
        for ch in range(3):
            total = total + g_ref[:, 11 + 3 * m + ch, :] * cot[6 + ch]
            out_ref[:, 11 + 3 * m + ch, :] = basis[m] * cot[6 + ch]
        basis_cot.append(total)
    extra = pull_basis(basis_cot)
    for f in range(3):
        grads[f] = grads[f] + extra[f]
    for f in range(11):
        out_ref[:, f, :] = grads[f]


def pull_blocks(req, back, gaussians, center):
    owned = gaussians.shape[0]
    return pl.pallas_call(
        functools.partial(pull_kernel, center),
        grid=(owned // UNIT,),
        in_specs=[
            pl.BlockSpec(req.shape, lambda i: (0, 0)),
            pl.BlockSpec(back.shape, lambda i: (0, 0)),
            pl.BlockSpec((UNIT, FIELDS, BLOCK), lambda i: (i, 0, 0)),
        ],
        out_specs=pl.BlockSpec((UNIT, FIELDS, BLOCK), lambda i: (i, 0, 0)),
        out_shape=jax.ShapeDtypeStruct(gaussians.shape, F32),
        scratch_shapes=[VMEM((owned, WIDE), F32)],
        name="pull",
    )(req, back, gaussians)


def extended(x, sides, width):
    for axis, dim in sides:
        size, length = (lax.axis_size(axis), x.shape[dim])
        up = [(i, (i + 1) % size) for i in range(size - 1)]
        down = [(j, i) for i, j in up]
        last = lax.slice_in_dim(x, length - width, length, axis=dim)
        first = lax.slice_in_dim(x, 0, width, axis=dim)
        before = lax.ppermute(last, axis, up)
        after = lax.ppermute(first, axis, down)
        x = jnp.concatenate([before, x, after], axis=dim)
    return x


def window_taps():
    offsets = np.arange(11, dtype=np.float32) - 5.0
    taps = np.exp(-offsets * offsets / 4.5)
    return taps / np.sum(taps)


def filtered(field, taps):
    rows = field.shape[-2] - 10
    cols = field.shape[-1] - 10
    sideways = sum((taps[shift] * field[..., :, shift : shift + cols] for shift in range(11)))
    return sum((taps[shift] * sideways[..., shift : shift + rows, :] for shift in range(11)))


def similarity(mean_a, mean_b, square_a, square_b, cross):
    var_a = square_a - mean_a * mean_a
    var_b = square_b - mean_b * mean_b
    covar = cross - mean_a * mean_b
    top = (2.0 * mean_a * mean_b + LUMA_TERM) * (2.0 * covar + CONTRAST_TERM)
    bottom = (mean_a * mean_a + mean_b * mean_b + LUMA_TERM) * (var_a + var_b + CONTRAST_TERM)
    return top / bottom


def moments(picture, goal, taps):
    return (
        filtered(picture, taps),
        filtered(goal, taps),
        filtered(picture * picture, taps),
        filtered(goal * goal, taps),
        filtered(picture * goal, taps),
    )


def per_device(gaussians, tile_lists, tile_counts, depth_order, target):
    across = lax.axis_size("tx")
    row_index = lax.axis_index("ty")
    col_index = lax.axis_index("tx")
    height = SIDE * lax.axis_size("ty")
    width = SIDE * across
    center = (0.5 * width, 0.5 * height)
    ranks = tile_lists.reshape(LMAX)
    count = tile_counts.reshape(1)
    place = jnp.stack([row_index * across, row_index, col_index]).astype(jnp.int32)
    table, req, slots = project_blocks(gaussians, ranks, count, depth_order, place, center, across)
    asked = lax.all_to_all(req, "tx", split_axis=0, concat_axis=0, tiled=True)
    local = asked[:, 0]
    served = table[jnp.maximum(local, 0)]
    recv = lax.all_to_all(served, "tx", split_axis=0, concat_axis=0, tiled=True)
    ahead, back = features()
    flat_image, light, color = render(slots, count, place, ahead, recv)
    image = flat_image.reshape(3, SIDE, SIDE)
    taps = window_taps()
    stacked = jnp.stack([image, target])
    framed = extended(stacked, (("ty", 2), ("tx", 3)), 5)
    maps = moments(framed[0], framed[1], taps)
    score, pull_score = jax.vjp(similarity, *maps)
    parts = pull_score(jnp.full_like(score, -STRUCT_WEIGHT))
    coeffs = jnp.stack([parts[0], parts[2], parts[4]])
    spread = extended(coeffs, (("ty", 2), ("tx", 3)), 5)
    smoothed = filtered(spread, taps)
    gap = image - target
    robust = jnp.sqrt(gap * gap + ROBUST_TERM)
    local_total = jnp.sum((1.0 - STRUCT_WEIGHT) * robust + STRUCT_WEIGHT * (1.0 - score))
    image_grad = (
        smoothed[0]
        + 2.0 * image * smoothed[1]
        + target * smoothed[2]
        + (1.0 - STRUCT_WEIGHT) * gap / robust
    )
    total = lax.psum(local_total, ("ty", "tx"))
    grads = render_gradient(
        slots, count, place, ahead, back, recv, light, color, image_grad.reshape(3, 8, BLOCK)
    )
    returned = lax.all_to_all(grads, "tx", split_axis=0, concat_axis=0, tiled=True)
    return pull_blocks(asked, returned, gaussians, center), total / (3.0 * height * width)


def solution(mesh):
    return jax.shard_map(
        per_device,
        mesh=mesh,
        in_specs=(
            P(("ty", "tx"), None, None),
            P("ty", "tx", None),
            P("ty", "tx"),
            P(),
            P(None, "ty", "tx"),
        ),
        out_specs=(P(("ty", "tx"), None, None), P()),
        check_vma=False,
    )
```

time: 727 us -> 227 us (0.31); the launches traced: 716 us -> 226 us
  other arithmetic: 297 us -> 4.36 us
  local copies, waits for them, and re-layouts: 104 us -> 15.7 us
  starting transfers between devices: 96.8 us -> 30.2 us
  matrix products: 61.6 us -> 0 us
  Pallas kernels: 0 us -> 59.8 us
  waiting for transfers between devices: 39 us -> 17 us
  loops' own time: 20.8 us -> 0 us
    another operation x63 -> x1, other arithmetic: 125 us -> 0.67 us  [per_device(): jnp.stack([row_index * across, row_index, col_index]).astype(jnp.int32)]
    dot_general x20 -> x0, matrix products: 61.6 us -> none  [composite(): jnp.dot(flat[6:9], weight, precision=lax.Precision.HIGHEST, preferred_ele...]
    pallas_call x0 -> x4, Pallas kernels: none -> 59.8 us  [the longest x1 27.3 us: render_gradient(): pl.pallas_call(backward_kernel, in_specs=[smem, smem, smem] + [vmem] * 6,...]
    all_to_all x2 -> x1, starting transfers between devices: 59.9 us -> 8.69 us  [per_device(): lax.all_to_all(grads, 'tx', split_axis=0, concat_axis=0, tiled=True)]
    reduce_sum x25 -> x0, other arithmetic: 46.5 us -> none  [the longest x10 26.6 us: composite(): return (color, jnp.sum(keep, axis=0))]
    add x6, other arithmetic: 43.4 us -> 1.87 us  [filtered(): sum((taps[shift] * field[..., :, shift:shift + cols] for shift in range(1...]
    mul x50 -> x0, other arithmetic: 29.5 us -> none  [the longest x30 25.3 us: composite(): alpha = (live * flat[5])[:, None] * jnp.exp(-0.5 * power)]
    another operation x49 -> x0, local copies, waits for them, and re-layouts: 27.3 us -> none
  transfers between devices with their start and end apart: 10 -> 9, of which waited for: 7 -> 5; matrix products, arithmetic and copies ran while one was open for 0% -> 0% of each run, Pallas kernels for 0% -> 0%
where the time goes in v1:
time: 227 us; the launch traced here: 226 us
  blocking collectives  95.6 us (42%)
  Pallas kernels  59.8 us (26%)
  starting transfers between devices  30.2 us (13%)
  waiting for transfers between devices  17 us (7%)
  local copies, waits for them, and re-layouts  15.7 us (7%)
  other arithmetic  4.36 us (2%)
  between operations  3.31 us (1%)
    psum x1, blocking collectives, per_device(): total = lax.psum(local_total, ('ty', 'tx'))  67.1 us
    pallas_call x1, Pallas kernels, render_gradient(): pl.pallas_call(backward_kernel, in_specs=[smem, smem, smem] + [vmem] * 6,...  27.3 us
    all_to_all x1, blocking collectives, per_device(): asked = lax.all_to_all(req, 'tx', split_axis=0, concat_axis=0, tiled=True)  15.1 us
    ppermute x4, starting transfers between devices, extended(): before = lax.ppermute(last, axis, up)  15.1 us
    ppermute x4, waiting for transfers between devices, extended(): after = lax.ppermute(first, axis, down)  14.7 us
    pallas_call x1, Pallas kernels, pull_blocks(): pl.pallas_call(functools.partial(pull_kernel, center), grid=(owned // UNI...  13.7 us
    all_to_all x1, blocking collectives, per_device(): recv = lax.all_to_all(served, 'tx', split_axis=0, concat_axis=0, tiled=True)  13.3 us
    pallas_call x1, Pallas kernels, project_blocks(): pl.pallas_call(functools.partial(project_kernel, owned, center), grid=(ow...  11.2 us
  transfers between devices with their start and end apart: 9, of which 5 were waited for; matrix products, arithmetic and copies ran while one was open for 0% of the time, Pallas kernels for 0%

profile of v1, /device:TPU:1, one launch (start us, length us, event | category | flops | bytes accessed | tf_op | source)
XLA Modules:
  0.0 225.9 jit_solution(6161949555004992887)
XLA Ops:
  1.3 5.2 %copy.12.g_ref = f32[96,59,128]{2,1,0:T(8,128)} copy(f32[96,59,128]{2,0,1:T(8,128)} %param.7) | data formatting | bytes 5799936 | tf_op args[0]
  7.1 11.2 %project.1 = (f32[96,1152]{1,0:T(8,128)}, s32[128,128]{1,0:T(8,128)}, s32[24]{0:T(128)}) custom-call(s32[24]{0:T(128)} %bitcast.64, s32[1]{0:T(128)} %bitcast.50.count, s32[12288]{0:T(1024)} %order.1, s32[3]{0:T(128)} %pad_add_fusion.place, f32[96,59,128]{2,1,0:T(8,128)} %copy.12.g_ref), custom_call_target="tpu_custom_call" | custom-call | tf_op jit(solution)/shard_map/project/pallas_call | solution.py:190
  18.3 15.1 %all_to_all.33 = s32[16,8,128]{2,1,0:T(8,128)S(1)} all-to-all(s32[16,8,128]{2,1,0:T(8,128)} %bitcast.63), channel_id=1, replica_groups=mesh['ty'=8,'tx'=16] {'tx'}, dimensions={0} | all-to-all | bytes 131072 | tf_op jit(solution)/shard_map/all_to_all | solution.py:581
  33.5 2.1 gather_fusion
  35.7 13.3 %all_to_all.34 = f32[16,8,1152]{2,1,0:T(8,128)} all-to-all(f32[16,8,1152]{2,1,0:T(8,128)S(1)} %bitcast.57), channel_id=1, replica_groups=mesh['ty'=8,'tx'=16] {'tx'}, dimensions={0} | all-to-all | bytes 1179648 | tf_op jit(solution)/shard_map/all_to_all | solution.py:584
  49.0 7.6 %render.1 = (f32[3,8,128]{2,1,0:T(8,128)}, f32[24,1024]{1,0:T(8,128)}, f32[3,24,1024]{2,1,0:T(8,128)}) custom-call(s32[24]{0:T(128)} %get-tuple-element.9.slot_ref, s32[1]{0:T(128)} %bitcast.51.count, s32[3]{0:T(128)} %pad_add_fusion.place, bf16[32,1024]{1,0:T(8,128)(2,1)} %constant.9.clone.ahead_ref, f32[128,1152]{1,0:T(8,128)} %bitcast.53), custom_call_target="tpu_custom_call" | custom-call | tf_op jit(solution)/shard_map/render/pallas_call | solution.py:323
  57.4 6.2 %collective-permute-start = (f32[2,3,5,32]{3,2,1,0:T(8,128)S(1)}, f32[2,3,5,32]{3,2,1,0:T(8,128)S(1)}, u32[]{:S(2)}, u32[]{:S(2)}) collective-permute-start(f32[2,3,5,32]{3,2,1,0:T(8,128)S(1)} %get-tuple-element.39), channel_id=1, source_target_pairs={{0,16},{16,32},{32,48},{48,64},{64,80},{80,96},{96,112},{1,17},{17... | collective-permute-start | bytes 11528 | tf_op jit(solution)/shard_map/ppermute | solution.py:532
  63.6 1.9 collective-permute-start.1
  65.5 3.2 %collective-permute-done.1 = f32[2,3,5,32]{3,2,1,0:T(8,128)S(1)} collective-permute-done((f32[2,3,5,32]{3,2,1,0:T(8,128)S(1)}, f32[2,3,5,32]{3,2,1,0:T(8,128)S(1)}, u32[]{:S(2)}, u32[]{:S(2)}) %collective-permute-start.1) | collective-permute-done | bytes 3872 | tf_op jit(solution)/shard_map/ppermute | solution.py:533
  68.8 2.2 collective-permute-start.2
  71.0 1.3 collective-permute-start.3
  73.1 4.1 %collective-permute-done.3 = f32[2,3,42,5]{3,2,1,0:T(8,128)S(1)} collective-permute-done((f32[2,3,42,5]{3,2,1,0:T(8,128)S(1)}, f32[2,3,42,5]{3,2,1,0:T(8,128)S(1)}, u32[]{:S(2)}, u32[]{:S(2)}) %collective-permute-start.3) | collective-permute-done | bytes 5072 | tf_op jit(solution)/shard_map/ppermute | solution.py:533
  79.8 4.3 %collective-permute-start.4 = (f32[3,3,5,32]{3,2,1,0:T(8,128)S(1)}, f32[3,3,5,32]{3,2,1,0:T(8,128)S(1)}, u32[]{:S(2)}, u32[]{:S(2)}) collective-permute-start(f32[3,3,5,32]{3,2,1,0:T(8,128)S(1)} %get-tuple-element.29), channel_id=1, source_target_pairs={{0,16},{16,32},{32,48},{48,64},{64,80},{80,96},{96,112},{1,17},{17... | collective-permute-start | bytes 17288 | tf_op jit(solution)/shard_map/ppermute | solution.py:532
  84.1 1.9 collective-permute-start.5
  86.0 3.3 %collective-permute-done.5 = f32[3,3,5,32]{3,2,1,0:T(8,128)S(1)} collective-permute-done((f32[3,3,5,32]{3,2,1,0:T(8,128)S(1)}, f32[3,3,5,32]{3,2,1,0:T(8,128)S(1)}, u32[]{:S(2)}, u32[]{:S(2)}) %collective-permute-start.5) | collective-permute-done | bytes 5792 | tf_op jit(solution)/shard_map/ppermute | solution.py:533
  89.5 2.4 %collective-permute-start.6 = (f32[3,3,42,5]{3,2,1,0:T(8,128)S(1)}, f32[3,3,42,5]{3,2,1,0:T(8,128)S(1)}, u32[]{:S(2)}, u32[]{:S(2)}) collective-permute-start(f32[3,3,42,5]{3,2,1,0:T(8,128)S(1)} %get-tuple-element.25), channel_id=1, source_target_pairs={{0,1},{1,2},{2,3},{3,4},{4,5},{5,6},{6,7},{7,8},{8,9},{9,10},{10,1... | collective-permute-start | bytes 22688 | tf_op jit(solution)/shard_map/ppermute | solution.py:532
  91.9 1.3 collective-permute-start.7
  93.2 2.2 collective-permute-done.6
  95.4 4.1 %collective-permute-done.7 = f32[3,3,42,5]{3,2,1,0:T(8,128)S(1)} collective-permute-done((f32[3,3,42,5]{3,2,1,0:T(8,128)S(1)}, f32[3,3,42,5]{3,2,1,0:T(8,128)S(1)}, u32[]{:S(2)}, u32[]{:S(2)}) %collective-permute-start.7) | collective-permute-done | bytes 7592 | tf_op jit(solution)/shard_map/ppermute | solution.py:533
  101.2 27.3 %render_gradient.1 = f32[128,1152]{1,0:T(8,128)} custom-call(s32[24]{0:T(128)} %get-tuple-element.9.slot_ref, s32[1]{0:T(128)} %bitcast.52.count, s32[3]{0:T(128)} %pad_add_fusion.place, bf16[32,1024]{1,0:T(8,128)(2,1)} %constant.9.clone.ahead_ref, bf16[16,1024]{1,0:T(8,128)(2,1)} %constant.10.clone.back_ref, f32[128,1152]{1,0:T(8,128)} %bitcast.54, ...), custom_call_target="tpu_custom_call" | custom-call | tf_op jit(solution)/shard_map/render_gradient/pallas_call | solution.py:450
  128.6 8.7 %all-to-all-start.2 = ((f32[16,8,1152]{2,1,0:T(8,128)}), f32[16,8,1152]{2,1,0:T(8,128)S(1)}, u32[]{:S(2)}, u32[]{:S(2)}) async-start(f32[16,8,1152]{2,1,0:T(8,128)} %bitcast.55), calls=%async_computation.2 | async-start | bytes 1179648 | tf_op jit(solution)/shard_map/all_to_all | solution.py:610
  137.3 67.1 %psum.7 = f32[]{:T(128)} all-reduce(f32[]{:T(128)} %get-tuple-element.18), channel_id=1, replica_groups=mesh['ty'=8,'tx'=16] {'ty','tx'}, use_global_device_ids=true, to_apply=%region_1.0 | all-reduce | flops 1 | bytes 8 | tf_op jit(solution)/shard_map/psum | solution.py:606
  205.9 13.7 %pull.1 = f32[96,59,128]{2,1,0:T(8,128)} custom-call(s32[128,128]{1,0:T(8,128)} %bitcast.62, f32[128,1152]{1,0:T(8,128)} %bitcast.56, f32[96,59,128]{2,1,0:T(8,128)} %copy.12.g_ref), custom_call_target="tpu_custom_call" | custom-call | tf_op jit(solution)/shard_map/pull/pallas_call | solution.py:510
  219.6 5.2 %copy.14 = f32[96,59,128]{2,0,1:T(8,128)} copy(f32[96,59,128]{2,1,0:T(8,128)} %pull.1) | data formatting | bytes 5799936
  (36 shorter events, 7.6 us)
Async XLA Ops:
  33.4 15.6 %copy-start.2 = (s32[16,8,128]{2,1,0:T(8,128)}, s32[16,8,128]{2,1,0:T(8,128)S(1)}, u32[]{:S(2)}) copy-start(s32[16,8,128]{2,1,0:T(8,128)S(1)} %all_to_all.33) | copy-start | bytes 196612
  33.5 23.8 %copy-start.1 = (f32[3,32,32]{2,1,0:T(8,128)S(1)}, f32[3,32,32]{2,1,0:T(8,128)}, u32[]{:S(2)}) copy-start(f32[3,32,32]{2,1,0:T(8,128)} %param.11) | copy-start | bytes 36868
  57.4 8.1 %collective-permute-start = (f32[2,3,5,32]{3,2,1,0:T(8,128)S(1)}, f32[2,3,5,32]{3,2,1,0:T(8,128)S(1)}, u32[]{:S(2)}, u32[]{:S(2)}) collective-permute-start(f32[2,3,5,32]{3,2,1,0:T(8,128)S(1)} %get-tuple-element.39), channel_id=1, source_target_pairs={{0,16},{16,32},{32,48},{48,64},{64,80},{80,96},{96,112},{1,17},{17... | collective-permute-start | bytes 11528 | tf_op jit(solution)/shard_map/ppermute | solution.py:532
  63.6 5.1 %collective-permute-start.1 = (f32[2,3,5,32]{3,2,1,0:T(8,128)S(1)}, f32[2,3,5,32]{3,2,1,0:T(8,128)S(1)}, u32[]{:S(2)}, u32[]{:S(2)}) collective-permute-start(f32[2,3,5,32]{3,2,1,0:T(8,128)S(1)} %get-tuple-element.40), channel_id=1, source_target_pairs={{16,0},{32,16},{48,32},{64,48},{80,64},{96,80},{112,96},{17,1},{33... | collective-permute-start | bytes 11528 | tf_op jit(solution)/shard_map/ppermute | solution.py:533
  68.8 4.3 %collective-permute-start.2 = (f32[2,3,42,5]{3,2,1,0:T(8,128)S(1)}, f32[2,3,42,5]{3,2,1,0:T(8,128)S(1)}, u32[]{:S(2)}, u32[]{:S(2)}) collective-permute-start(f32[2,3,42,5]{3,2,1,0:T(8,128)S(1)} %get-tuple-element.37), channel_id=1, source_target_pairs={{0,1},{1,2},{2,3},{3,4},{4,5},{5,6},{6,7},{7,8},{8,9},{9,10},{10,1... | collective-permute-start | bytes 15128 | tf_op jit(solution)/shard_map/ppermute | solution.py:532
  71.0 6.2 %collective-permute-start.3 = (f32[2,3,42,5]{3,2,1,0:T(8,128)S(1)}, f32[2,3,42,5]{3,2,1,0:T(8,128)S(1)}, u32[]{:S(2)}, u32[]{:S(2)}) collective-permute-start(f32[2,3,42,5]{3,2,1,0:T(8,128)S(1)} %get-tuple-element.38), channel_id=1, source_target_pairs={{1,0},{2,1},{3,2},{4,3},{5,4},{6,5},{7,6},{8,7},{9,8},{10,9},{11,1... | collective-permute-start | bytes 15128 | tf_op jit(solution)/shard_map/ppermute | solution.py:533
  79.8 6.2 %collective-permute-start.4 = (f32[3,3,5,32]{3,2,1,0:T(8,128)S(1)}, f32[3,3,5,32]{3,2,1,0:T(8,128)S(1)}, u32[]{:S(2)}, u32[]{:S(2)}) collective-permute-start(f32[3,3,5,32]{3,2,1,0:T(8,128)S(1)} %get-tuple-element.29), channel_id=1, source_target_pairs={{0,16},{16,32},{32,48},{48,64},{64,80},{80,96},{96,112},{1,17},{17... | collective-permute-start | bytes 17288 | tf_op jit(solution)/shard_map/ppermute | solution.py:532
  84.1 5.3 %collective-permute-start.5 = (f32[3,3,5,32]{3,2,1,0:T(8,128)S(1)}, f32[3,3,5,32]{3,2,1,0:T(8,128)S(1)}, u32[]{:S(2)}, u32[]{:S(2)}) collective-permute-start(f32[3,3,5,32]{3,2,1,0:T(8,128)S(1)} %get-tuple-element.30), channel_id=1, source_target_pairs={{16,0},{32,16},{48,32},{64,48},{80,64},{96,80},{112,96},{17,1},{33... | collective-permute-start | bytes 17288 | tf_op jit(solution)/shard_map/ppermute | solution.py:533
  89.5 5.9 %collective-permute-start.6 = (f32[3,3,42,5]{3,2,1,0:T(8,128)S(1)}, f32[3,3,42,5]{3,2,1,0:T(8,128)S(1)}, u32[]{:S(2)}, u32[]{:S(2)}) collective-permute-start(f32[3,3,42,5]{3,2,1,0:T(8,128)S(1)} %get-tuple-element.25), channel_id=1, source_target_pairs={{0,1},{1,2},{2,3},{3,4},{4,5},{5,6},{6,7},{7,8},{8,9},{9,10},{10,1... | collective-permute-start | bytes 22688 | tf_op jit(solution)/shard_map/ppermute | solution.py:532
  91.9 7.6 %collective-permute-start.7 = (f32[3,3,42,5]{3,2,1,0:T(8,128)S(1)}, f32[3,3,42,5]{3,2,1,0:T(8,128)S(1)}, u32[]{:S(2)}, u32[]{:S(2)}) collective-permute-start(f32[3,3,42,5]{3,2,1,0:T(8,128)S(1)} %get-tuple-element.26), channel_id=1, source_target_pairs={{1,0},{2,1},{3,2},{4,3},{5,4},{6,5},{7,6},{8,7},{9,8},{10,9},{11,1... | collective-permute-start | bytes 22688 | tf_op jit(solution)/shard_map/ppermute | solution.py:533
  128.6 76.5 %all-to-all-start.2 = ((f32[16,8,1152]{2,1,0:T(8,128)}), f32[16,8,1152]{2,1,0:T(8,128)S(1)}, u32[]{:S(2)}, u32[]{:S(2)}) async-start(f32[16,8,1152]{2,1,0:T(8,128)} %bitcast.55), calls=%async_computation.2 | async-start | bytes 1179648 | tf_op jit(solution)/shard_map/all_to_all | solution.py:610
  205.1 0.8 copy-start

commit v2 on v1

--- a/solution.py
+++ b/solution.py
@@ -22,7 +22,10 @@
 CHUNKS = ROWS // CHUNK
 STEPS = CHUNK // UNIT
 FIELDS = 59
-WIDE = 9 * BLOCK
+NUMBERS = 9
+WIDE = NUMBERS * BLOCK
+PACK = CAP * NUMBERS
+PER_STEP = 24
 
 FOCAL = 1000.0
 LOW_PASS = 0.3
@@ -148,7 +151,7 @@
     def _():
         req_ref[...] = jnp.full_like(req_ref, -1)
         first = place[0]
-        for o in range(req_ref.shape[0] // SLOT):
+        for o in range(req_ref.shape[0]):
             used[o] = 0
 
         def put(k, carry):
@@ -159,46 +162,48 @@
 
             @pl.when(k < count[0])
             def _():
-                row = owner * SLOT + used[owner]
-                used[owner] = used[owner] + 1
-                slot_ref[k] = row
-                req_ref[pl.ds(row, 1), :] = jnp.full((1, BLOCK), local, jnp.int32)
+                turn = used[owner]
+                used[owner] = turn + 1
+                slot_ref[k] = owner * SLOT + turn
+                req_ref[owner, pl.ds(turn, 1), :] = jnp.full((1, BLOCK), local, jnp.int32)
 
             @pl.when(k >= count[0])
             def _():
-                slot_ref[k] = SLOT - 1
+                slot_ref[k] = 0
 
             return carry
 
         lax.fori_loop(0, LMAX, put, 0)
 
-    field = [g_ref[:, f, :] for f in range(11)]
-    shape = shape_of(center[0], center[1], *field)
-    basis = basis_of(*field[:3])
-    for f in range(6):
-        out_ref[:, f * BLOCK : (f + 1) * BLOCK] = shape[f]
-    for ch in range(3):
-        color = jnp.full((UNIT, BLOCK), 0.5, F32)
-        for m in range(16):
-            color = color + g_ref[:, 11 + 3 * m + ch, :] * basis[m]
-        out_ref[:, (6 + ch) * BLOCK : (7 + ch) * BLOCK] = color
+    for part in range(PER_STEP // UNIT):
+        rows = slice(part * UNIT, (part + 1) * UNIT)
+        field = [g_ref[f, rows, :] for f in range(11)]
+        shape = shape_of(center[0], center[1], *field)
+        basis = basis_of(*field[:3])
+        for f in range(6):
+            out_ref[rows, f * BLOCK : (f + 1) * BLOCK] = shape[f]
+        for ch in range(3):
+            color = jnp.full((UNIT, BLOCK), 0.5, F32)
+            for m in range(16):
+                color = color + g_ref[11 + 3 * m + ch, rows, :] * basis[m]
+            out_ref[rows, (6 + ch) * BLOCK : (7 + ch) * BLOCK] = color
 
 
 def project_blocks(gaussians, ranks, count, order, place, center, peers):
-    owned = gaussians.shape[0]
+    owned = gaussians.shape[1]
     smem = pl.BlockSpec(memory_space=pltpu.SMEM)
     return pl.pallas_call(
         functools.partial(project_kernel, owned, center),
-        grid=(owned // UNIT,),
-        in_specs=[smem, smem, smem, smem, pl.BlockSpec((UNIT, FIELDS, BLOCK), lambda i: (i, 0, 0))],
+        grid=(owned // PER_STEP,),
+        in_specs=[smem, smem, smem, smem, pl.BlockSpec((FIELDS, PER_STEP, BLOCK), lambda i: (0, i, 0))],
         out_specs=[
-            pl.BlockSpec((UNIT, WIDE), lambda i: (i, 0)),
-            pl.BlockSpec((peers * SLOT, BLOCK), lambda i: (0, 0)),
+            pl.BlockSpec((PER_STEP, WIDE), lambda i: (i, 0)),
+            pl.BlockSpec((peers, SLOT, BLOCK), lambda i: (0, 0, 0)),
             smem,
         ],
         out_shape=[
             jax.ShapeDtypeStruct((owned, WIDE), F32),
-            jax.ShapeDtypeStruct((peers * SLOT, BLOCK), jnp.int32),
+            jax.ShapeDtypeStruct((peers, SLOT, BLOCK), jnp.int32),
             jax.ShapeDtypeStruct((LMAX,), jnp.int32),
         ],
         scratch_shapes=[pltpu.SMEM((peers,), jnp.int32)],
@@ -221,7 +226,9 @@
 
 def load_entries(slot_ref, recv_ref, ent_ref):
     for k in range(LMAX):
-        ent_ref[k : k + 1, :] = recv_ref[pl.ds(slot_ref[k], 1), :]
+        slot = slot_ref[k]
+        held = recv_ref[slot // SLOT, pl.ds(lax.rem(slot, SLOT) * NUMBERS, NUMBERS), :]
+        ent_ref[pl.ds(k, NUMBERS, stride=LMAX), :] = held
 
 
 def build_rows(place, count, ent_ref, field_ref, row_ref):
@@ -231,9 +238,8 @@
     mid_y = mid_y * SIDE + (SIDE // 2 + 0.5)
     field_ref[...] = jnp.zeros_like(field_ref)
     for unit in range(UNITS):
-        rows = slice(unit * UNIT, (unit + 1) * UNIT)
         u, v, a, b, c, log_o, r0, r1, r2 = [
-            ent_ref[rows, f * BLOCK : (f + 1) * BLOCK] for f in range(9)
+            ent_ref[f * LMAX + unit * UNIT : f * LMAX + (unit + 1) * UNIT, :] for f in range(NUMBERS)
         ]
         entry = lax.broadcasted_iota(jnp.int32, (UNIT, BLOCK), 0) + unit * UNIT
         live = entry < count[0]
@@ -331,7 +337,7 @@
         ],
         scratch_shapes=[
             VMEM((UNITS * ROWS, BLOCK), F32),
-            VMEM((LMAX, WIDE), F32),
+            VMEM((NUMBERS * LMAX, BLOCK), F32),
             VMEM((32 * UNIT, BLOCK), F32),
             VMEM((CHUNK, PIX), F32),
             VMEM((CHUNK, PIX), F32),
@@ -419,12 +425,11 @@
     mid_x = place[2].astype(F32) * SIDE + (SIDE // 2 + 0.5)
     mid_y = place[1].astype(F32) * SIDE + (SIDE // 2 + 0.5)
     for unit in range(UNITS):
-        rows = slice(unit * UNIT, (unit + 1) * UNIT)
         for s in range(UNIT):
             table = moment_ref[pl.ds(unit * ROWS + s, BLOCK, stride=UNIT), :].T
             field_ref[pl.ds(s, 16, stride=UNIT), :] = table[:16]
         m = [field_ref[f * UNIT : (f + 1) * UNIT, :] for f in range(14)]
-        u, v, a, b, c = [ent_ref[rows, f * BLOCK : (f + 1) * BLOCK] for f in range(5)]
+        u, v, a, b, c = [ent_ref[f * LMAX + unit * UNIT : f * LMAX + (unit + 1) * UNIT, :] for f in range(5)]
         du, dv = u - mid_x, v - mid_y
         near_x, near_y = m[1] - du * m[0], m[2] - dv * m[0]
         values = [
@@ -439,9 +444,14 @@
             m[10] + m[13],
         ]
         for f, value in enumerate(values):
-            result_ref[rows, f * BLOCK : (f + 1) * BLOCK] = value
+            result_ref[f * LMAX + unit * UNIT : f * LMAX + (unit + 1) * UNIT, :] = value
     for k in range(LMAX):
-        out_ref[pl.ds(slot_ref[k], 1), :] = result_ref[k : k + 1, :]
+
+        @pl.when(k < count[0])
+        def _():
+            slot = slot_ref[k]
+            row = pl.ds(lax.rem(slot, SLOT) * NUMBERS, NUMBERS)
+            out_ref[slot // SLOT, row, :] = result_ref[pl.ds(k, NUMBERS, stride=LMAX), :]
 
 
 def render_gradient(slots, count, place, ahead, back, recv, light, color, grad):
@@ -454,7 +464,7 @@
         out_shape=jax.ShapeDtypeStruct(recv.shape, F32),
         scratch_shapes=[
             VMEM((UNITS * ROWS, BLOCK), F32),
-            VMEM((LMAX, WIDE), F32),
+            VMEM((NUMBERS * LMAX, BLOCK), F32),
             VMEM((32 * UNIT, BLOCK), F32),
             VMEM((ROWS, PIX), F32),
             VMEM((ROWS, PIX), F32),
@@ -462,90 +472,253 @@
             VMEM((LMAX, PIX), F32),
             VMEM((LMAX, PIX), F32),
             VMEM((UNITS * ROWS, BLOCK), F32),
-            VMEM((LMAX, WIDE), F32),
+            VMEM((NUMBERS * LMAX, BLOCK), F32),
         ],
         name="render_gradient",
     )(slots, count, place, ahead, back, recv, light, color, grad)
 
 
-def pull_kernel(center, req_ref, back_ref, g_ref, out_ref, dense_ref):
+def pull_kernel(center, scale, req_ref, back_ref, total_ref, g_ref, out_ref, loss_ref, dense_ref):
     step = pl.program_id(0)
 
     @pl.when(step == 0)
     def _():
+        loss_ref[0] = jnp.sum(total_ref[...]) * scale
         owned = dense_ref.shape[0]
-        req = req_ref[...]
+        req = jnp.concatenate([req_ref[:, turn, :] for turn in range(CAP)], axis=0)
         lane = lax.broadcasted_iota(jnp.int32, req.shape, 1)
         chosen = jnp.where(req == lane, 1.0, 0.0).T[:owned].astype(BF16)
         asked = req >= 0
-        for f in range(9):
+        for f in range(NUMBERS):
             cols = slice(f * BLOCK, (f + 1) * BLOCK)
-            value = jnp.where(asked, back_ref[:, cols], 0.0)
+            value = jnp.concatenate([back_ref[:, turn * NUMBERS + f, :] for turn in range(CAP)], axis=0)
+            value = jnp.where(asked, value, 0.0)
             dense_ref[:, cols] = sum(
                 jnp.dot(chosen, part.astype(BF16), preferred_element_type=F32) for part in pieces(value, 3)
             )
 
-    rows = pl.ds(pl.multiple_of(step * UNIT, UNIT), UNIT)
-    cot = [dense_ref[rows, f * BLOCK : (f + 1) * BLOCK] for f in range(9)]
-    field = [g_ref[:, f, :] for f in range(11)]
-    _, pull = jax.vjp(functools.partial(shape_of, center[0], center[1]), *field)
-    grads = list(pull(tuple(cot[:6])))
-    basis, pull_basis = jax.vjp(basis_of, *field[:3])
-    basis_cot = []
-    for m in range(16):
-        total = jnp.zeros((UNIT, BLOCK), F32)
-        for ch in range(3):
-            total = total + g_ref[:, 11 + 3 * m + ch, :] * cot[6 + ch]
-            out_ref[:, 11 + 3 * m + ch, :] = basis[m] * cot[6 + ch]
-        basis_cot.append(total)
-    extra = pull_basis(basis_cot)
-    for f in range(3):
-        grads[f] = grads[f] + extra[f]
-    for f in range(11):
-        out_ref[:, f, :] = grads[f]
-
-
-def pull_blocks(req, back, gaussians, center):
-    owned = gaussians.shape[0]
+    for part in range(PER_STEP // UNIT):
+        here = slice(part * UNIT, (part + 1) * UNIT)
+        rows = pl.ds(pl.multiple_of(step * PER_STEP + part * UNIT, UNIT), UNIT)
+        cot = [dense_ref[rows, f * BLOCK : (f + 1) * BLOCK] for f in range(9)]
+        field = [g_ref[f, here, :] for f in range(11)]
+        _, pull = jax.vjp(functools.partial(shape_of, center[0], center[1]), *field)
+        grads = list(pull(tuple(cot[:6])))
+        basis, pull_basis = jax.vjp(basis_of, *field[:3])
+        basis_cot = []
+        for m in range(16):
+            total = jnp.zeros((UNIT, BLOCK), F32)
+            for ch in range(3):
+                total = total + g_ref[11 + 3 * m + ch, here, :] * cot[6 + ch]
+                out_ref[11 + 3 * m + ch, here, :] = basis[m] * cot[6 + ch]
+            basis_cot.append(total)
+        extra = pull_basis(basis_cot)
+        for f in range(3):
+            grads[f] = grads[f] + extra[f]
+        for f in range(11):
+            out_ref[f, here, :] = grads[f]
+
+
+def pull_blocks(req, back, total, gaussians, center, scale):
+    owned = gaussians.shape[1]
     return pl.pallas_call(
-        functools.partial(pull_kernel, center),
-        grid=(owned // UNIT,),
+        functools.partial(pull_kernel, center, scale),
+        grid=(owned // PER_STEP,),
         in_specs=[
-            pl.BlockSpec(req.shape, lambda i: (0, 0)),
-            pl.BlockSpec(back.shape, lambda i: (0, 0)),
-            pl.BlockSpec((UNIT, FIELDS, BLOCK), lambda i: (i, 0, 0)),
-        ],
-        out_specs=pl.BlockSpec((UNIT, FIELDS, BLOCK), lambda i: (i, 0, 0)),
-        out_shape=jax.ShapeDtypeStruct(gaussians.shape, F32),
+            pl.BlockSpec(req.shape, lambda i: (0, 0, 0)),
+            pl.BlockSpec(back.shape, lambda i: (0, 0, 0)),
+            pl.BlockSpec(total.shape, lambda i: (0, 0)),
+            pl.BlockSpec((FIELDS, PER_STEP, BLOCK), lambda i: (0, i, 0)),
+        ],
+        out_specs=[
+            pl.BlockSpec((FIELDS, PER_STEP, BLOCK), lambda i: (0, i, 0)),
+            pl.BlockSpec(memory_space=pltpu.SMEM),
+        ],
+        out_shape=[
+            jax.ShapeDtypeStruct(gaussians.shape, F32),
+            jax.ShapeDtypeStruct((1,), F32),
+        ],
         scratch_shapes=[VMEM((owned, WIDE), F32)],
         name="pull",
-    )(req, back, gaussians)
-
-
-def extended(x, sides, width):
-    for axis, dim in sides:
-        size, length = (lax.axis_size(axis), x.shape[dim])
-        up = [(i, (i + 1) % size) for i in range(size - 1)]
-        down = [(j, i) for i, j in up]
-        last = lax.slice_in_dim(x, length - width, length, axis=dim)
-        first = lax.slice_in_dim(x, 0, width, axis=dim)
-        before = lax.ppermute(last, axis, up)
-        after = lax.ppermute(first, axis, down)
-        x = jnp.concatenate([before, x, after], axis=dim)
-    return x
+    )(req, back, total, gaussians)
+
+
+MESH = pl.DeviceIdType.MESH
+NEAR = [(dy, dx) for dy in (-1, 0, 1) for dx in (-1, 0, 1) if (dy, dx) != (0, 0)]
+
+
+def greet(targets):
+    barrier = pltpu.get_barrier_semaphore()
+    for target in targets:
+        pl.semaphore_signal(barrier, inc=1, device_id=target, device_id_type=MESH)
+    pl.semaphore_wait(barrier, len(targets))
+
+
+def row_peers(n):
+    me = lax.axis_index("tx")
+    return me, [lax.rem(me + d, n) for d in range(1, n)]
+
+
+def serve_kernel(n, req_ref, table_ref, asked_ref, recv_ref, served_ref, req_send, req_recv, data_send, data_recv):
+    me, peers = row_peers(n)
+    greet([{"tx": peer} for peer in peers])
+    asks = []
+    for d, peer in enumerate(peers):
+        asks.append(
+            pltpu.make_async_remote_copy(
+                src_ref=req_ref.at[peer],
+                dst_ref=asked_ref.at[me],
+                send_sem=req_send.at[d],
+                recv_sem=req_recv.at[d],
+                device_id={"tx": peer},
+                device_id_type=MESH,
+            )
+        )
+        asks[-1].start()
+    asked_ref[me] = req_ref[me]
+    parts = [part.astype(BF16) for part in pieces(table_ref[...], 3)]
+    for copy in asks:
+        copy.wait_recv()
+    owned = table_ref.shape[0]
+    asked = jnp.concatenate([asked_ref[:, turn, :] for turn in range(CAP)], axis=0)
+    lane = lax.broadcasted_iota(jnp.int32, asked.shape, 1)
+    chosen = jnp.where(asked == lane, 1.0, 0.0)[:, :owned].astype(BF16)
+    served = sum(jnp.dot(chosen, part, preferred_element_type=F32) for part in parts)
+    for turn in range(CAP):
+        for f in range(NUMBERS):
+            value = served[turn * n : (turn + 1) * n, f * BLOCK : (f + 1) * BLOCK]
+            served_ref[:, turn * NUMBERS + f, :] = value
+    sends = []
+    for d, peer in enumerate(peers):
+        sends.append(
+            pltpu.make_async_remote_copy(
+                src_ref=served_ref.at[peer],
+                dst_ref=recv_ref.at[me],
+                send_sem=data_send.at[d],
+                recv_sem=data_recv.at[d],
+                device_id={"tx": peer},
+                device_id_type=MESH,
+            )
+        )
+        sends[-1].start()
+    recv_ref[me] = served_ref[me]
+    for copy in sends:
+        copy.wait_recv()
+    for copy in asks:
+        copy.wait_send()
+    for copy in sends:
+        copy.wait_send()
+
+
+def serve(req, table, n):
+    vmem = pl.BlockSpec(memory_space=pltpu.VMEM)
+    dma = pltpu.SemaphoreType.DMA((n - 1,))
+    return pl.pallas_call(
+        functools.partial(serve_kernel, n),
+        in_specs=[vmem, vmem],
+        out_specs=[vmem, vmem],
+        out_shape=[
+            jax.ShapeDtypeStruct(req.shape, jnp.int32),
+            jax.ShapeDtypeStruct((n, PACK, BLOCK), F32),
+        ],
+        scratch_shapes=[VMEM((n, PACK, BLOCK), F32), dma, dma, dma, dma],
+        compiler_params=pltpu.CompilerParams(collective_id=0, has_side_effects=True),
+        name="serve",
+    )(req, table)
+
+
+def reply_kernel(n, rows, grad_ref, part_ref, back_ref, total_ref, column_ref, sum_ref, line_ref,
+                 data_send, data_recv, col_send, col_recv, row_send, row_recv):
+    me, peers = row_peers(n)
+    mine = lax.axis_index("ty")
+    others = [lax.rem(mine + d, rows) for d in range(1, rows)]
+    greet([{"tx": peer} for peer in peers] + [{"ty": other} for other in others])
+    columns = []
+    for d, other in enumerate(others):
+        columns.append(
+            pltpu.make_async_remote_copy(
+                src_ref=part_ref,
+                dst_ref=column_ref.at[mine],
+                send_sem=col_send.at[d],
+                recv_sem=col_recv.at[d],
+                device_id={"ty": other},
+                device_id_type=MESH,
+            )
+        )
+        columns[-1].start()
+    sends = []
+    for d, peer in enumerate(peers):
+        sends.append(
+            pltpu.make_async_remote_copy(
+                src_ref=grad_ref.at[peer],
+                dst_ref=back_ref.at[me],
+                send_sem=data_send.at[d],
+                recv_sem=data_recv.at[d],
+                device_id={"tx": peer},
+                device_id_type=MESH,
+            )
+        )
+        sends[-1].start()
+    column_ref[mine] = part_ref[...]
+    back_ref[me] = grad_ref[me]
+    for copy in columns:
+        copy.wait_recv()
+    sum_ref[...] = sum(column_ref[r] for r in range(rows))
+    lines = []
+    for d, peer in enumerate(peers):
+        lines.append(
+            pltpu.make_async_remote_copy(
+                src_ref=sum_ref,
+                dst_ref=line_ref.at[me],
+                send_sem=row_send.at[d],
+                recv_sem=row_recv.at[d],
+                device_id={"tx": peer},
+                device_id_type=MESH,
+            )
+        )
+        lines[-1].start()
+    line_ref[me] = sum_ref[...]
+    for copy in lines:
+        copy.wait_recv()
+    total_ref[...] = sum(line_ref[c] for c in range(n))
+    for copy in sends:
+        copy.wait_recv()
+    for copy in columns + sends + lines:
+        copy.wait_send()
+
+
+def reply(grads, part, n, rows):
+    vmem = pl.BlockSpec(memory_space=pltpu.VMEM)
+    wide = pltpu.SemaphoreType.DMA((n - 1,))
+    tall = pltpu.SemaphoreType.DMA((rows - 1,))
+    return pl.pallas_call(
+        functools.partial(reply_kernel, n, rows),
+        in_specs=[vmem, vmem],
+        out_specs=[vmem, vmem],
+        out_shape=[
+            jax.ShapeDtypeStruct(grads.shape, F32),
+            jax.ShapeDtypeStruct(part.shape, F32),
+        ],
+        scratch_shapes=[
+            VMEM((rows,) + part.shape, F32),
+            VMEM(part.shape, F32),
+            VMEM((n,) + part.shape, F32),
+            wide,
+            wide,
+            tall,
+            tall,
+            wide,
+            wide,
+        ],
+        compiler_params=pltpu.CompilerParams(collective_id=1, has_side_effects=True),
+        name="reply",
+    )(grads, part)
 
 
 def window_taps():
-    offsets = np.arange(11, dtype=np.float32) - 5.0
-    taps = np.exp(-offsets * offsets / 4.5)
-    return taps / np.sum(taps)
-
-
-def filtered(field, taps):
-    rows = field.shape[-2] - 10
-    cols = field.shape[-1] - 10
-    sideways = sum((taps[shift] * field[..., :, shift : shift + cols] for shift in range(11)))
-    return sum((taps[shift] * sideways[..., shift : shift + rows, :] for shift in range(11)))
+    offsets = np.arange(11, dtype=np.float32) - np.float32(5.0)
+    taps = np.exp(-offsets * offsets / np.float32(4.5))
+    return [float(tap) for tap in taps / np.sum(taps)]
 
 
 def similarity(mean_a, mean_b, square_a, square_b, cross):
@@ -557,58 +730,171 @@
     return top / bottom
 
 
-def moments(picture, goal, taps):
-    return (
-        filtered(picture, taps),
-        filtered(goal, taps),
-        filtered(picture * picture, taps),
-        filtered(goal * goal, taps),
-        filtered(picture * goal, taps),
-    )
+EXT = 3 * SIDE
+TOP = SIDE - 8
+TALL = SIDE + 16
+
+
+def symmetric(taps, part):
+    total = taps[5] * part(5)
+    for k in range(5):
+        total = total + taps[k] * (part(k) + part(10 - k))
+    return total
+
+
+def filter_rows(taps, ref, start, rows):
+    tall = symmetric(taps, lambda k: ref[start + k : start + k + rows, :])
+    return symmetric(taps, lambda k: tall if k == 5 else pltpu.roll(tall, (5 - k) % BLOCK, 1))
+
+
+def similarity_kernel(cols, rows, image_ref, goal_ref, grad_ref, part_ref, near_ref, pic_ref, aim_ref,
+                      prod_ref, coef_ref, flat_ref, image_send, image_recv, goal_send, goal_recv):
+    row, col = lax.axis_index("ty"), lax.axis_index("tx")
+    targets = [
+        {"ty": lax.rem(row + dy + rows, rows), "tx": lax.rem(col + dx + cols, cols)} for dy, dx in NEAR
+    ]
+    greet(targets)
+    copies = []
+    for d, target in enumerate(targets):
+        for src, half, send, recv in (
+            (image_ref, 0, image_send, image_recv),
+            (goal_ref, 1, goal_send, goal_recv),
+        ):
+            copies.append(
+                pltpu.make_async_remote_copy(
+                    src_ref=src,
+                    dst_ref=near_ref.at[d, half],
+                    send_sem=send.at[d],
+                    recv_sem=recv.at[d],
+                    device_id=target,
+                    device_id_type=MESH,
+                )
+            )
+            copies[-1].start()
+    lane = lax.broadcasted_iota(jnp.int32, (8, BLOCK), 1)
+    wide = lane + (col - 1) * SIDE
+    inside = (wide >= 0) & (wide < cols * SIDE) & (lane < EXT)
+    for copy in copies:
+        copy.wait_recv()
+    for dy in (-1, 0, 1):
+        high = jnp.zeros((8, BLOCK), jnp.int32) + (row + dy)
+        there = inside & (high >= 0) & (high < rows)
+        for half, own, out in ((0, image_ref, pic_ref), (1, goal_ref, aim_ref)):
+            for ch in range(3):
+                tiles = []
+                for dx in (-1, 0, 1):
+                    if (dy, dx) == (0, 0):
+                        tiles.append(own[ch])
+                    else:
+                        tiles.append(near_ref[NEAR.index((-dy, -dx)), half, ch])
+                for q in range(4):
+                    moved = []
+                    for place, tile in enumerate(tiles):
+                        shift = (SIDE * (place - q)) % BLOCK
+                        moved.append(pltpu.roll(tile, shift, 1) if shift else tile)
+                    value = jnp.where(lane < SIDE, moved[0], jnp.where(lane < 2 * SIDE, moved[1], moved[2]))
+                    value = jnp.where(there, value, 0.0)
+                    out[pl.ds(ch * EXT + (dy + 1) * SIDE + q, 8, stride=4), :] = value
+    taps = window_taps()
+    high = lax.broadcasted_iota(jnp.int32, (TALL, BLOCK), 0) + (row * SIDE + TOP - SIDE)
+    long = lax.broadcasted_iota(jnp.int32, (TALL, BLOCK), 1) + (col - 1) * SIDE
+    scored = (high >= 0) & (high < rows * SIDE) & (long >= 0) & (long < cols * SIDE)
+    middle = lax.broadcasted_iota(jnp.int32, (SIDE, BLOCK), 1)
+    middle = (middle >= SIDE) & (middle < 2 * SIDE)
+    part = jnp.zeros((SIDE, BLOCK), F32)
+    for ch in range(3):
+        base = ch * EXT
+        picture = pic_ref[base : base + EXT, :]
+        goal = aim_ref[base : base + EXT, :]
+        prod_ref[0:EXT, :] = picture * picture
+        prod_ref[EXT : 2 * EXT, :] = goal * goal
+        prod_ref[2 * EXT : 3 * EXT, :] = picture * goal
+        maps = [
+            filter_rows(taps, ref, start + TOP - 5, TALL)
+            for ref, start in (
+                (pic_ref, base),
+                (aim_ref, base),
+                (prod_ref, 0),
+                (prod_ref, EXT),
+                (prod_ref, 2 * EXT),
+            )
+        ]
+        score, pull_score = jax.vjp(similarity, *maps)
+        parts = pull_score(jnp.full_like(score, -STRUCT_WEIGHT))
+        for i, which in enumerate((0, 2, 4)):
+            coef_ref[i * TALL : (i + 1) * TALL, :] = jnp.where(scored, parts[which], 0.0)
+        smooth = [filter_rows(taps, coef_ref, i * TALL + SIDE - TOP - 5, SIDE) for i in range(3)]
+        image = pic_ref[base + SIDE : base + 2 * SIDE, :]
+        target = aim_ref[base + SIDE : base + 2 * SIDE, :]
+        gap = image - target
+        robust = jnp.sqrt(gap * gap + ROBUST_TERM)
+        own_score = score[SIDE - TOP : 2 * SIDE - TOP, :]
+        part = part + (1.0 - STRUCT_WEIGHT) * robust + STRUCT_WEIGHT * (1.0 - own_score)
+        flat_ref[...] = (
+            smooth[0]
+            + 2.0 * image * smooth[1]
+            + target * smooth[2]
+            + (1.0 - STRUCT_WEIGHT) * gap / robust
+        )
+        value = jnp.zeros((8, BLOCK), F32)
+        for q in range(4):
+            line = flat_ref[pl.ds(q, 8, stride=4), :]
+            shift = (SIDE * (q - 1)) % BLOCK
+            line = pltpu.roll(line, shift, 1) if shift else line
+            value = jnp.where((lane >= SIDE * q) & (lane < SIDE * (q + 1)), line, value)
+        grad_ref[ch] = value
+    part = jnp.where(middle, part, 0.0)
+    part_ref[...] = part[0:8] + part[8:16] + part[16:24] + part[24:32]
+    for copy in copies:
+        copy.wait_send()
+
+
+def image_gradient(image, goal, cols, rows):
+    vmem = pl.BlockSpec(memory_space=pltpu.VMEM)
+    dma = pltpu.SemaphoreType.DMA((len(NEAR),))
+    return pl.pallas_call(
+        functools.partial(similarity_kernel, cols, rows),
+        in_specs=[vmem, vmem],
+        out_specs=[vmem, vmem],
+        out_shape=[jax.ShapeDtypeStruct(image.shape, F32), jax.ShapeDtypeStruct((8, BLOCK), F32)],
+        scratch_shapes=[
+            VMEM((len(NEAR), 2) + image.shape, F32),
+            VMEM((3 * EXT, BLOCK), F32),
+            VMEM((3 * EXT, BLOCK), F32),
+            VMEM((3 * EXT, BLOCK), F32),
+            VMEM((3 * TALL, BLOCK), F32),
+            VMEM((SIDE, BLOCK), F32),
+            dma,
+            dma,
+            dma,
+            dma,
+        ],
+        compiler_params=pltpu.CompilerParams(collective_id=2, has_side_effects=True),
+        name="image_gradient",
+    )(image, goal)
 
 
 def per_device(gaussians, tile_lists, tile_counts, depth_order, target):
     across = lax.axis_size("tx")
+    down = lax.axis_size("ty")
     row_index = lax.axis_index("ty")
     col_index = lax.axis_index("tx")
-    height = SIDE * lax.axis_size("ty")
+    height = SIDE * down
     width = SIDE * across
     center = (0.5 * width, 0.5 * height)
     ranks = tile_lists.reshape(LMAX)
     count = tile_counts.reshape(1)
     place = jnp.stack([row_index * across, row_index, col_index]).astype(jnp.int32)
-    table, req, slots = project_blocks(gaussians, ranks, count, depth_order, place, center, across)
-    asked = lax.all_to_all(req, "tx", split_axis=0, concat_axis=0, tiled=True)
-    local = asked[:, 0]
-    served = table[jnp.maximum(local, 0)]
-    recv = lax.all_to_all(served, "tx", split_axis=0, concat_axis=0, tiled=True)
+    by_field = gaussians.transpose(1, 0, 2)
+    table, req, slots = project_blocks(by_field, ranks, count, depth_order, place, center, across)
+    asked, recv = serve(req, table, across)
     ahead, back = features()
-    flat_image, light, color = render(slots, count, place, ahead, recv)
-    image = flat_image.reshape(3, SIDE, SIDE)
-    taps = window_taps()
-    stacked = jnp.stack([image, target])
-    framed = extended(stacked, (("ty", 2), ("tx", 3)), 5)
-    maps = moments(framed[0], framed[1], taps)
-    score, pull_score = jax.vjp(similarity, *maps)
-    parts = pull_score(jnp.full_like(score, -STRUCT_WEIGHT))
-    coeffs = jnp.stack([parts[0], parts[2], parts[4]])
-    spread = extended(coeffs, (("ty", 2), ("tx", 3)), 5)
-    smoothed = filtered(spread, taps)
-    gap = image - target
-    robust = jnp.sqrt(gap * gap + ROBUST_TERM)
-    local_total = jnp.sum((1.0 - STRUCT_WEIGHT) * robust + STRUCT_WEIGHT * (1.0 - score))
-    image_grad = (
-        smoothed[0]
-        + 2.0 * image * smoothed[1]
-        + target * smoothed[2]
-        + (1.0 - STRUCT_WEIGHT) * gap / robust
-    )
-    total = lax.psum(local_total, ("ty", "tx"))
-    grads = render_gradient(
-        slots, count, place, ahead, back, recv, light, color, image_grad.reshape(3, 8, BLOCK)
-    )
-    returned = lax.all_to_all(grads, "tx", split_axis=0, concat_axis=0, tiled=True)
-    return pull_blocks(asked, returned, gaussians, center), total / (3.0 * height * width)
+    image, light, color = render(slots, count, place, ahead, recv)
+    image_grad, part = image_gradient(image, target.reshape(3, 8, BLOCK), across, down)
+    grads = render_gradient(slots, count, place, ahead, back, recv, light, color, image_grad)
+    returned, total = reply(grads, part, across, down)
+    pulled, loss = pull_blocks(asked, returned, total, by_field, center, 1.0 / (3.0 * height * width))
+    return pulled.transpose(1, 0, 2), loss.reshape(())
 
 
 def solution(mesh):

time: 227 us -> 95.9 us (0.42)
  blocking collectives: 95.6 us -> 0 us
  Pallas kernels: 59.8 us -> 92 us
  starting transfers between devices: 30.2 us -> 0 us
  waiting for transfers between devices: 17 us -> 0 us
  local copies, waits for them, and re-layouts: 15.7 us -> 1.48 us
  other arithmetic: 4.36 us -> 0.61 us
    psum x1 -> x0, blocking collectives: 67.1 us -> none  [per_device(): total = lax.psum(local_total, ('ty', 'tx'))]
    pallas_call x1 -> x4, Pallas kernels: 13.7 us -> 51.7 us  [the longest x1 18.4 us: serve(): pl.pallas_call(functools.partial(serve_kernel, n), in_specs=[vmem, vmem],...]
    all_to_all x2 -> x0, blocking collectives: 28.4 us -> none  [the longest x1 15.1 us: per_device(): asked = lax.all_to_all(req, 'tx', split_axis=0, concat_axis=0, tiled=True)]
    ppermute x8 -> x0, starting transfers between devices: 21.5 us -> none  [the longest x4 15.1 us: extended(): before = lax.ppermute(last, axis, up)]
    ppermute x8 -> x0, waiting for transfers between devices: 17 us -> none  [the longest x4 14.7 us: extended(): after = lax.ppermute(first, axis, down)]
    unnamed x8 -> x0, local copies, waits for them, and re-layouts: 11.1 us -> none
    all_to_all x1 -> x0, starting transfers between devices: 8.69 us -> none  [per_device(): lax.all_to_all(grads, 'tx', split_axis=0, concat_axis=0, tiled=True)]
    pallas_call x1, Pallas kernels: 11.2 us -> 5.13 us  [project_blocks(): pl.pallas_call(functools.partial(project_kernel, owned, center), grid=(ow...]
  transfers between devices with their start and end apart: 9 -> 0, of which waited for: 5 -> 0; matrix products, arithmetic and copies ran while one was open for 0% -> 0% of each run, Pallas kernels for 0% -> 0%
where the time goes in v2:
time: 95.9 us; the launch traced here: 95.4 us
  Pallas kernels  92 us (96%)
  local copies, waits for them, and re-layouts  1.48 us (2%)
  between operations  1.31 us (1%)
    pallas_call x1, Pallas kernels, render_gradient(): pl.pallas_call(backward_kernel, in_specs=[smem, smem, smem] + [vmem] * 6,...  27.6 us
    pallas_call x1, Pallas kernels, serve(): pl.pallas_call(functools.partial(serve_kernel, n), in_specs=[vmem, vmem],...  18.4 us
    pallas_call x1, Pallas kernels, image_gradient(): pl.pallas_call(functools.partial(similarity_kernel, cols, rows), in_specs...  14.7 us
    pallas_call x1, Pallas kernels, reply(): pl.pallas_call(functools.partial(reply_kernel, n, rows), in_specs=[vmem,...  13.4 us
    pallas_call x1, Pallas kernels, render(): pl.pallas_call(forward_kernel, in_specs=[smem, smem, smem, vmem, vmem], o...  7.55 us
    pallas_call x1, Pallas kernels, pull_blocks(): pl.pallas_call(functools.partial(pull_kernel, center, scale), grid=(owned...  5.17 us
    pallas_call x1, Pallas kernels, project_blocks(): pl.pallas_call(functools.partial(project_kernel, owned, center), grid=(ow...  5.13 us

profile of v2, /device:TPU:1, one launch (start us, length us, event | category | flops | bytes accessed | tf_op | source)
XLA Modules:
  0.0 95.4 jit_solution(17373860538150418200)
XLA Ops:
  1.3 0.6 pad_add_fusion.place
  1.9 1.5 %reshape.18.goal_ref = f32[3,8,128]{2,1,0:T(8,128)} reshape(f32[3,32,32]{2,1,0:T(8,128)} %param.11) | data formatting | bytes 24576 | tf_op jit(solution)/shard_map/reshape | solution.py:893
  3.4 5.1 %project.1 = (f32[96,1152]{1,0:T(8,128)}, s32[16,8,128]{2,1,0:T(8,128)}, s32[24]{0:T(128)}) custom-call(s32[24]{0:T(128)} %bitcast.13, s32[1]{0:T(128)} %bitcast.8.count, s32[12288]{0:T(1024)} %order.1, s32[3]{0:T(128)} %pad_add_fusion.place, f32[59,96,128]{2,1,0:T(8,128)} %bitcast.11), custom_call_target="tpu_custom_call" | custom-call | tf_op jit(solution)/shard_map/project/pallas_call | solution.py:195
  8.5 18.4 %serve.1 = (s32[16,8,128]{2,1,0:T(8,128)}, f32[16,27,128]{2,1,0:T(8,128)}) custom-call(s32[16,8,128]{2,1,0:T(8,128)} %get-tuple-element.16.req_ref, f32[96,1152]{1,0:T(8,128)} %get-tuple-element.17.table_ref), custom_call_target="tpu_custom_call" | custom-call | tf_op jit(solution)/shard_map/serve/pallas_call | solution.py:616
  26.9 7.5 %render.1 = (f32[3,8,128]{2,1,0:T(8,128)}, f32[24,1024]{1,0:T(8,128)}, f32[3,24,1024]{2,1,0:T(8,128)}) custom-call(s32[24]{0:T(128)} %get-tuple-element.19.slot_ref, s32[1]{0:T(128)} %bitcast.9.count, s32[3]{0:T(128)} %pad_add_fusion.place, bf16[32,1024]{1,0:T(8,128)(2,1)} %constant.15.clone.ahead_ref, f32[16,27,128]{2,1,0:T(8,128)} %get-tuple-element.20.recv_ref), custom_call_target="tpu_custom_call" | custom-call | tf_op jit(solution)/shard_map/render/pallas_call | solution.py:329
  34.5 14.7 %image_gradient.1 = (f32[3,8,128]{2,1,0:T(8,128)}, f32[8,128]{1,0:T(8,128)}) custom-call(f32[3,8,128]{2,1,0:T(8,128)} %get-tuple-element.23.image_ref, f32[3,8,128]{2,1,0:T(8,128)} %reshape.18.goal_ref), custom_call_target="tpu_custom_call" | custom-call | tf_op jit(solution)/shard_map/image_gradient/pallas_call | solution.py:855
  49.2 27.6 %render_gradient.1.grad_ref = f32[16,27,128]{2,1,0:T(8,128)} custom-call(s32[24]{0:T(128)} %get-tuple-element.19.slot_ref, s32[1]{0:T(128)} %bitcast.10.count, s32[3]{0:T(128)} %pad_add_fusion.place, bf16[32,1024]{1,0:T(8,128)(2,1)} %constant.15.clone.ahead_ref, bf16[16,1024]{1,0:T(8,128)(2,1)} %constant.16.clone.back_ref, ...), custom_call_target="tpu_custom_call" | custom-call | tf_op jit(solution)/shard_map/render_gradient/pallas_call | solution.py:460
  76.8 13.4 %reply.1 = (f32[16,27,128]{2,1,0:T(8,128)}, f32[8,128]{1,0:T(8,128)}) custom-call(f32[16,27,128]{2,1,0:T(8,128)} %render_gradient.1.grad_ref, f32[8,128]{1,0:T(8,128)} %get-tuple-element.25.part_ref), custom_call_target="tpu_custom_call" | custom-call | tf_op jit(solution)/shard_map/reply/pallas_call | solution.py:694
  90.3 5.2 %pull.1 = (f32[59,96,128]{2,1,0:T(8,128)}, f32[1]{0:T(128)}) custom-call(s32[16,8,128]{2,1,0:T(8,128)} %get-tuple-element.18.req_ref, f32[16,27,128]{2,1,0:T(8,128)} %get-tuple-element.26.back_ref, f32[8,128]{1,0:T(8,128)} %get-tuple-element.27.total_ref, f32[59,96,128]{2,1,0:T(8,128)} %bitcast.12), custom_call_target="tpu_custom_call" | custom-call | tf_op jit(solution)/shard_map/pull/pallas_call | solution.py:524
